TPU v7x, 512 devices: a whole 4x4x16 slice. The times are simulated.
512 devices in a mesh: row: 32 (over z_lo, y, core), col: 16 (over x, z_hi).
Axes of the slice: x: 4, y: 4, z: 16 (z_hi: 4, z_lo: 4; z = z_hi * 4 + z_lo), core: 2. Of those that a mesh axis runs over, the one named last changes fastest.
Arguments:
- features: bfloat16 [65536, 256], P(('row', 'col')), may hold values from -6 to 6
- tile_values: bfloat16 [32, 16, 32, 128, 128], P('row', 'col'), may hold values from -0.109375 to 0.109375
- tile_rows: int32 [32, 16, 32], P('row', 'col'), may hold values from 0 to 15, as said below
- tile_cols: int32 [32, 16, 32], P('row', 'col'), may hold values from 0 to 31
- tile_count: int32 [32, 16], P('row', 'col'), may hold values from 1 to 32, as said below
- weight: bfloat16 [256, 256], replicated, may hold values from -0.375 to 0.375
- out_grad: bfloat16 [65536, 256], P(('row', 'col')), may hold values from -6 to 6
Outputs:
- activated: bfloat16 [65536, 256], P(('row', 'col'))
- feature_grad: bfloat16 [65536, 256], P(('row', 'col'))
- weight_grad: float32 [256, 256], replicated
Inputs may be any that keep to these rules, and one draw needn't show every extreme that they name: Within one grid cell the pairs (tile_rows, tile_cols) of all 32 slots are distinct. `tile_count`: some grid cell has all 32 slots live.
All inputs are finite; a program needn't handle non-finite values.
Results may differ from a plain program's by a relative error of at most 0.023.
Values may be sent and summed in bfloat16 or wider, within the bound.
No kernel may reach another device: no remote copies, remote signals or barrier semaphores. Data moves between devices by JAX's collectives and lax.ppermute only.
A program may use at most 64 MiB of HBM per device.

v0:
```python
import math

import jax
import jax.numpy as jnp
from jax import lax
from jax.sharding import PartitionSpec as P


def gelu_value(preact):
    return jax.nn.gelu(preact, approximate=True)


def gelu_backward(preact, upstream):
    _, pullback = jax.vjp(gelu_value, preact)
    return pullback(upstream)[0]


def combine_tiles(tiles, read_ids, write_ids, live_count, source_blocks, dest_tiles, transposed):
    slot_total = tiles.shape[0]
    tile_size = tiles.shape[1]
    feat_width = source_blocks.shape[2]
    group = math.gcd(slot_total, 32)
    slot_index = jnp.arange(group, dtype=jnp.int32)

    def one_group(group_index, running):
        offset = group_index * group
        live_part = slot_index + offset < live_count
        gathered = jnp.take(source_blocks, read_ids, axis=0)
        if transposed:
            products = jnp.einsum(
                "tab,taf->tbf", tiles, gathered, preferred_element_type=jnp.float32
            )
        else:
            products = jnp.einsum(
                "tab,tbf->taf", tiles, gathered, preferred_element_type=jnp.float32
            )
        products = jnp.where(live_part[:, None, None], products, jnp.float32(0.0))
        return running.at[write_ids].add(products)

    initial = jnp.zeros((dest_tiles, tile_size, feat_width), jnp.float32)
    groups_live = (live_count + (group - 1)) // group
    return lax.fori_loop(jnp.int32(0), groups_live, one_group, initial)


def body(features, tile_values, tile_rows, tile_cols, tile_count, weight, out_grad):
    tiles = tile_values[0, 0]
    row_ids = tile_rows[0, 0]
    col_ids = tile_cols[0, 0]
    live_count = tile_count[0, 0]
    tile_size = tiles.shape[1]
    node_rows, feat_width = features.shape
    grid_rows = lax.axis_size("row")
    grid_cols = lax.axis_size("col")
    row_tiles = grid_cols * node_rows // tile_size
    col_tiles = grid_rows * node_rows // tile_size
    projected = jnp.dot(features, weight, preferred_element_type=jnp.float32).astype(jnp.bfloat16)
    column_block = lax.all_gather(projected, "row", axis=0, tiled=True).reshape(
        col_tiles, tile_size, feat_width
    )
    partial_value = combine_tiles(
        tiles, col_ids, row_ids, live_count, column_block, row_tiles, False
    )
    partial_value = partial_value.reshape(row_tiles * tile_size, feat_width)
    own_rows = lax.psum_scatter(
        partial_value.astype(jnp.bfloat16), "col", scatter_dimension=0, tiled=True
    ).astype(jnp.float32)
    activated = gelu_value(own_rows).astype(jnp.bfloat16)
    cotangent = gelu_backward(own_rows, out_grad.astype(jnp.float32)).astype(jnp.bfloat16)
    cotangent_block = lax.all_gather(cotangent, "col", axis=0, tiled=True)
    row_blocks = cotangent_block.reshape(row_tiles, tile_size, feat_width)
    back_terms = combine_tiles(tiles, row_ids, col_ids, live_count, row_blocks, col_tiles, True)
    back_terms = back_terms.reshape(col_tiles * tile_size, feat_width)
    pulled = lax.psum_scatter(
        back_terms.astype(jnp.bfloat16), "row", scatter_dimension=0, tiled=True
    )
    weight_term = lax.dot_general(
        features, pulled, (((0,), (0,)), ((), ())), preferred_element_type=jnp.float32
    )
    total_nodes = node_rows * grid_rows * grid_cols
    weight_grad = lax.psum(weight_term, ("row", "col")) * total_nodes ** (-0.5)
    feature_grad = lax.dot_general(
        pulled, weight, (((1,), (1,)), ((), ())), preferred_element_type=jnp.float32
    ).astype(jnp.bfloat16)
    return (activated, feature_grad, weight_grad)


def solution(mesh):
    placed = (
        P(("row", "col"), None),
        P("row", "col", None, None, None),
        P("row", "col", None),
        P("row", "col", None),
        P("row", "col"),
        P(),
        P(("row", "col"), None),
    )
    return jax.shard_map(
        body,
        mesh=mesh,
        in_specs=placed,
        out_specs=(P(("row", "col"), None), P(("row", "col"), None), P()),
        check_vma=False,
    )
```

profile of v0, /device:TPU:10, one launch (start us, length us, event | category | flops | bytes accessed | tf_op | source)
XLA Modules:
  0.0 945.9 jit_solution(3820917195681366197)
XLA Ops:
  7.2 0.8 copy-done
  8.1 1.6 convolution_convert_fusion.1
  10.5 0.7 fusion.28
  11.1 68.6 %all-gather.3.cloned.1.call-done = bf16[4096,256]{1,0:T(8,128)(2,1)} async-done(((bf16[128,256]{1,0:T(8,128)(2,1)}), bf16[4096,256]{1,0:T(8,128)(2,1)}) %all-gather.3.cloned.1.call-update) | async-done | bytes 2097168 | tf_op jit(solution)/shard_map/all_gather | solution.py:57
  79.7 2.3 gather_fusion.1
  82.0 2.9 copy.17
  84.9 0.2 broadcast_in_dim.59
  85.1 1.0 copy-done.2
  86.1 17.1 %while.24 = (s32[]{:T(128)}, f32[16,128,256]{2,1,0:T(8,128)S(1)}, s32[]{:T(128)}, s32[32]{0:T(128)S(1)}, s32[]{:T(128)}, /*index=5*/s32[32]{0:T(128)S(1)}, bf16[...) while((s32[]{:T(128)}, f32[16,128,256]{2,1,0:T(8,128)S(1)}, ...), condition=%wide.region_2.3_spmd.clone, body=%wide.region_0.2_spmd.clone.sunk | while | flops 271581536 | bytes 28312312 | solution.py:42
  86.1 0.7 compare_and_fusion.4
  86.8 4.3 select_bitcast_fusion.4
  91.1 5.6 copy.22
  96.7 6.5 scatter_fusion
  103.2 1.1 convert_element_type.31
  104.4 0.0 all-gather.5.cloned.1.call-start
  104.4 113.4 %reduce-scatter.3.cloned.1.call-done = bf16[128,256]{1,0:T(8,128)(2,1)} async-done(((bf16[2048,256]{1,0:T(8,128)(2,1)}), bf16[128,256]{1,0:T(8,128)(2,1)}) %reduce-scatter.3.cloned.1.call-update) | async-done | bytes 65552 | tf_op jit(solution)/shard_map/reduce_scatter | solution.py:64
  217.8 1.6 fusion.20
  219.5 74.8 %all-gather.5.cloned.1.call-done = bf16[2048,256]{1,0:T(8,128)(2,1)} async-done(((bf16[128,256]{1,0:T(8,128)(2,1)}), bf16[2048,256]{1,0:T(8,128)(2,1)}) %all-gather.5.cloned.1.call-update) | async-done | bytes 1048592 | tf_op jit(solution)/shard_map/all_gather | solution.py:69
  294.2 2.5 broadcast_in_dim.60
  296.7 21.2 %while.25 = (s32[]{:T(128)}, f32[32,128,256]{2,1,0:T(8,128)}, s32[]{:T(128)}, s32[32]{0:T(128)S(1)}, s32[]{:T(128)}, /*index=5*/s32[32]{0:T(128)S(1)}, bf16[16,1...) while((s32[]{:T(128)}, f32[32,128,256]{2,1,0:T(8,128)}, s32[]{:T(128)}, ...), condition=%wide.region_6.7_spmd.clone, body=%wide.region_4.6_spmd.clone.sunk | while | flops 271582656 | bytes 32511224 | solution.py:42
  296.7 0.7 compare_and_fusion.5
  297.4 0.7 gather_fusion
  298.1 4.2 select_bitcast_fusion.5
  302.3 5.6 copy.23
  307.9 10.0 %scatter_fusion.1 = f32[32,128,256]{2,1,0:T(8,128)} fusion(f32[32,128,256]{2,1,0:T(8,128)} %get-tuple-element.407, s32[32]{0:T(128)S(1)} %get-tuple-element.362, f32[32,128,256]{2,1,0:T(8,128)} %copy.23), kind=kCustom, calls=%fused_computation.3.clone.clone.1 | custom fusion | flops 1048576 | bytes 12583040 | tf_op jit(solution)/shard_map/while/body/scatter-add | solution.py:38
  317.9 3.8 convert_element_type.37
  321.8 142.2 %reduce-scatter.5.cloned.1.call-done = bf16[128,256]{1,0:T(8,128)(2,1)} async-done(((bf16[4096,256]{1,0:T(8,128)(2,1)}), bf16[128,256]{1,0:T(8,128)(2,1)}) %reduce-scatter.5.cloned.1.call-update) | async-done | bytes 65552 | tf_op jit(solution)/shard_map/reduce_scatter | solution.py:73
  464.0 1.8 convolution_bitcast_fusion
  465.8 1.7 convolution_convert_fusion
  467.5 470.1 %all-reduce.2.cloned.1.call-done = f32[256,256]{0,1:T(8,128)} async-done(((f32[256,256]{0,1:T(8,128)}), f32[256,256]{0,1:T(8,128)}) %all-reduce.2.cloned.1.call-update) | async-done | bytes 262160 | tf_op jit(solution)/shard_map/psum | solution.py:80
  937.6 1.0 broadcast_multiply_fusion
  938.6 0.8 copy.18
  (25 shorter events, 0.3 us)
Async XLA Ops:
  7.2 0.9 copy-start
  7.2 72.5 %all-gather.3.cloned.1.call-start = ((), (), s32[]{:S(2)}) async-start(), calls=%async_computation.2 | async-start | bytes 2162688 | tf_op jit(solution)/shard_map/all_gather | solution.py:57
  9.7 208.1 %reduce-scatter.3.cloned.1.call-start = ((), (), s32[]{:S(2)}) async-start(), calls=%async_computation.3 | async-start | bytes 1114112 | tf_op jit(solution)/shard_map/reduce_scatter | solution.py:64
  84.9 1.2 copy-start.2
  84.9 1.2 copy-start.5
  84.9 1.2 copy-start.6
  103.2 114.6 %copy-start.4 = (bf16[128,256]{1,0:T(8,128)(2,1)S(1)}, bf16[128,256]{1,0:T(8,128)(2,1)}, u32[]{:S(2)}) copy-start(bf16[128,256]{1,0:T(8,128)(2,1)} %param.17) | copy-start | bytes 196612
  104.4 189.9 %all-gather.5.cloned.1.call-start = ((), (), s32[]{:S(2)}) async-start(), calls=%async_computation.4 | async-start | bytes 1114112 | tf_op jit(solution)/shard_map/all_gather | solution.py:69
  219.4 244.6 %reduce-scatter.5.cloned.1.call-start = ((), (), s32[]{:S(2)}) async-start(), calls=%async_computation.5 | async-start | bytes 2162688 | tf_op jit(solution)/shard_map/reduce_scatter | solution.py:73
  294.2 2.5 copy-start.1
  321.7 142.3 %copy-start.3 = (bf16[128,256]{1,0:T(8,128)(2,1)S(1)}, bf16[128,256]{1,0:T(8,128)(2,1)}, u32[]{:S(2)}) copy-start(bf16[128,256]{1,0:T(8,128)(2,1)} %param.11) | copy-start | bytes 196612
  321.7 615.9 %all-reduce.2.cloned.1.call-start = ((), (), s32[]{:S(2)}) async-start(), calls=%async_computation.6 | async-start | bytes 524288 | tf_op jit(solution)/shard_map/psum | solution.py:80
Sparse Core Ops, SparseCore 0:
  10.7 68.9 all-gather.2
  104.5 113.2 reduce-scatter.2
  221.4 72.8 all-gather.4
  321.8 142.1 reduce-scatter.4
  469.9 467.6 all-reduce.1
where the time goes:
time: 947 us; the launch traced here: 946 us
  waiting for transfers between devices  869 us (92%)
  other arithmetic  25.9 us (3%)
  local copies, waits for them, and re-layouts  22.5 us (2%)
  between operations  14.5 us (2%)
  matrix products  13.6 us (1%)
    psum x1, waiting for transfers between devices, body(): weight_grad = lax.psum(weight_term, ('row', 'col')) * total_nodes ** (-0.5)  470 us
    reduce_scatter x1, waiting for transfers between devices, body(): lax.psum_scatter(back_terms.astype(jnp.bfloat16), 'row', scatter_dimensio...  142 us
    reduce_scatter x1, waiting for transfers between devices, body(): lax.psum_scatter(partial_value.astype(jnp.bfloat16), 'col', scatter_dimen...  113 us
    all_gather x1, waiting for transfers between devices, body(): cotangent_block = lax.all_gather(cotangent, 'col', axis=0, tiled=True)  74.8 us
    all_gather x1, waiting for transfers between devices, body(): lax.all_gather(projected, 'row', axis=0, tiled=True)  68.6 us
  transfers between devices with their start and end apart: 5, of which 5 were waited for; matrix products, arithmetic and copies ran while one was open for 0% of the time, Pallas kernels for 0%

commit v1 on v0

v1 whole, which is shorter than its diff:
```python
import functools

import jax
import jax.numpy as jnp
from jax import lax
from jax.experimental import pallas as pl
from jax.experimental.pallas import tpu as pltpu
from jax.sharding import Mesh, PartitionSpec as P

F32 = jnp.float32
BF16 = jnp.bfloat16
AXES = ("zl", "y", "c", "x", "zh")
SIZES = (4, 4, 2, 4, 4)
T = 128
F = 256
UNROLL = 4

VMEM = pl.BlockSpec(memory_space=pltpu.VMEM)
SMEM = pl.BlockSpec(memory_space=pltpu.SMEM)


def call(kernel, out_shapes, in_specs, args, flops, scratch=()):
    nbytes = sum(a.size * a.dtype.itemsize for a in args)
    nbytes += sum(s.size * s.dtype.itemsize for s in out_shapes)
    return pl.pallas_call(
        kernel,
        out_shape=out_shapes,
        in_specs=in_specs,
        out_specs=tuple(VMEM for _ in out_shapes),
        scratch_shapes=list(scratch),
        compiler_params=pltpu.CompilerParams(vmem_limit_bytes=24 * 2**20),
        cost_estimate=pl.CostEstimate(flops=flops, bytes_accessed=nbytes, transcendentals=0),
    )(*args)


def sds(*shape, dtype=BF16):
    return jax.ShapeDtypeStruct(shape, dtype)


def dot(a, b, da, db):
    return lax.dot_general(a, b, (((da,), (db,)), ((), ())), preferred_element_type=F32)


def total(ref, *index):
    terms = [ref[(k,) + index].astype(F32) for k in range(ref.shape[0])]
    while len(terms) > 1:
        terms = [a + b for a, b in zip(terms[::2], terms[1::2])]
    return terms[0]


def split(v):
    hi = v.astype(BF16)
    return hi, (v - hi.astype(F32)).astype(BF16)


def over_slots(count, step):
    def group(g, carry):
        for k in range(UNROLL):
            s = g * UNROLL + k
            step(s, s < count)
        return carry

    lax.fori_loop(0, (count + UNROLL - 1) // UNROLL, group, 0)


def forward_kernel(rows, cols, count, me, tiles, own, other, out, acc):
    acc[...] = jnp.zeros_like(acc)
    mine = me[0]

    def step(s, live):
        r, a = rows[s], cols[s]
        k = (a // 2) % 4 * 4 + a // 8
        source = jnp.where(a % 2 == mine, own[k], other[k])
        tile = jnp.where(live, tiles[s], jnp.zeros((), BF16))
        acc[r] += dot(tile, source, 1, 0)

    over_slots(count[0], step)
    out[...] = acc[...].astype(BF16)


def sum_kernel(parts, out):
    out[...] = total(parts).astype(BF16)


def gelu_kernel(parts, weight, upstream, activated, cot, wterm):
    z = total(parts).astype(BF16)
    v = dot(z, weight[...], 1, 0)
    k = 0.7978845608028654
    v2 = v * v
    t = jnp.tanh(k * (v + 0.044715 * (v2 * v)))
    cdf = 0.5 * (1.0 + t)
    activated[...] = (v * cdf).astype(BF16)
    slope = cdf + 0.5 * v * (1.0 - t * t) * (k * (1.0 + 3 * 0.044715 * v2))
    d = (upstream[...].astype(F32) * slope).astype(BF16)
    cot[...] = d
    wterm[...] = dot(z, d, 0, 0).astype(BF16)


def pack_zh_kernel(wparts, cot, out):
    hi, lo = split(total(wparts))
    tail = jnp.concatenate([hi, lo], axis=0)
    for d in range(4):
        out[d, :T] = cot[...]
        out[d, T:] = tail


def pack_x_kernel(parts, out):
    w = total(parts, slice(T, T + 16))
    hi, lo = split(w[:8] + w[8:])
    tail = jnp.concatenate([hi, lo], axis=0)
    for d in range(4):
        for z in range(4):
            out[d, z * T : (z + 1) * T] = parts[z, :T]
        out[d, 4 * T :] = tail


def backward_kernel(rows, cols, count, me, tiles, cots, own, send, acc):
    acc[...] = jnp.zeros_like(acc)
    mine = me[0]

    def step(s, live):
        r, a = rows[s], cols[s]
        k = a % 2 * 16 + (a // 2) % 4 * 4 + a // 8
        source = cots[r // 4, pl.ds(pl.multiple_of(r % 4 * T, T), T)]
        tile = jnp.where(live, tiles[s], jnp.zeros((), BF16))
        acc[k] += dot(tile, source, 0, 0)

    over_slots(count[0], step)
    keep = mine * 16
    give = 16 - keep
    for k in range(16):
        own[k * T : (k + 1) * T] = acc[keep + k].astype(BF16)
        send[k * T : (k + 1) * T] = acc[give + k].astype(BF16)
    w = total(cots, slice(4 * T, 4 * T + 16))
    w = (w[:8] + w[8:]).astype(BF16)
    w = jnp.concatenate([w, w], axis=0)
    own[16 * T :] = w
    send[16 * T :] = w


def pack_y_kernel(me, own, got, out):
    for y in range(4):
        block = slice(y * 4 * T, (y + 1) * 4 * T)
        out[y, : 4 * T] = (own[block].astype(F32) + got[block].astype(F32)).astype(BF16)
    a = own[16 * T :].astype(F32)
    b = got[16 * T :].astype(F32)
    row = lax.broadcasted_iota(jnp.int32, (16, F), 0)
    tail = jnp.where(row // 8 == me[0], a, b).astype(BF16)
    for y in range(4):
        out[y, 4 * T :] = tail


def pack_zl_kernel(parts, out):
    for d in range(4):
        out[d, :T] = total(parts, slice(d * T, (d + 1) * T)).astype(BF16)
        for y in range(4):
            out[d, T + 16 * y : T + 16 * (y + 1)] = parts[y, 4 * T :]


def last_kernel(scale, parts, weight, feature_grad, weight_grad):
    pulled = total(parts, slice(0, T)).astype(BF16)
    feature_grad[...] = dot(pulled, weight[...], 1, 1).astype(BF16)
    for z in range(4):
        weight_grad[z * 64 : (z + 1) * 64] = parts[z, T:].astype(F32) * scale


def exchange(v, axis):
    return lax.all_to_all(v, axis, 0, 0)


def swap(v):
    return lax.ppermute(v, "c", [(0, 1), (1, 0)])


def body(features, tile_values, tile_rows, tile_cols, tile_count, weight, out_grad):
    tiles = tile_values[0, 0]
    rows, cols, count = tile_rows[0, 0], tile_cols[0, 0], tile_count[0]
    me = lax.axis_index("c").astype(jnp.int32).reshape(1)
    slots = tiles.shape[0]
    tile_flops = slots * 2 * T * T * F

    got = exchange(jnp.broadcast_to(features, (4, T, F)), "zl").reshape(4 * T, F)
    got = exchange(jnp.broadcast_to(got, (4, 4 * T, F)), "y").reshape(16, T, F)
    other = swap(got)

    (partial,) = call(
        forward_kernel,
        (sds(16, T, F),),
        [SMEM] * 4 + [VMEM] * 3,
        (rows, cols, count, me, tiles, got, other),
        tile_flops,
        [pltpu.VMEM((16, T, F), F32)],
    )
    parts = exchange(partial.reshape(4, 4 * T, F), "x")
    (summed,) = call(sum_kernel, (sds(4 * T, F),), [VMEM], (parts,), 2**20)
    parts = exchange(summed.reshape(4, T, F), "zh")
    activated, cot, wterm = call(
        gelu_kernel,
        (sds(T, F), sds(T, F), sds(F, F)),
        [VMEM] * 3,
        (parts, weight, out_grad),
        8 * T * F * F,
    )
    wparts = exchange(wterm.reshape(32, 8, F), ("zl", "y", "c"))

    (packed,) = call(pack_zh_kernel, (sds(4, T + 16, F),), [VMEM] * 2, (wparts, cot), 2**20)
    parts = exchange(packed, "zh")
    (packed,) = call(pack_x_kernel, (sds(4, 4 * T + 16, F),), [VMEM], (parts,), 2**20)
    cots = exchange(packed, "x")

    own, send = call(
        backward_kernel,
        (sds(16 * T + 16, F), sds(16 * T + 16, F)),
        [SMEM] * 4 + [VMEM] * 2,
        (rows, cols, count, me, tiles, cots),
        tile_flops,
        [pltpu.VMEM((32, T, F), F32)],
    )
    recv = swap(send)
    (packed,) = call(
        pack_y_kernel, (sds(4, 4 * T + 16, F),), [SMEM] + [VMEM] * 2, (me, own, recv), 2**20
    )
    parts = exchange(packed, "y")
    (packed,) = call(pack_zl_kernel, (sds(4, T + 64, F),), [VMEM], (parts,), 2**20)
    parts = exchange(packed, "zl")
    scale = float(T * 512) ** -0.5
    feature_grad, weight_grad = call(
        functools.partial(last_kernel, scale),
        (sds(T, F), sds(F, F, dtype=F32)),
        [VMEM] * 2,
        (parts, weight),
        2 * T * F * F,
    )
    return activated, feature_grad, weight_grad


def solution(mesh):
    fine = Mesh(mesh.devices.reshape(SIZES), AXES)
    row, col = AXES[:3], AXES[3:]
    placed = (
        P(AXES, None),
        P(row, col, None, None, None),
        P(row, col, None),
        P(row, col, None),
        P(row, col),
        P(),
        P(AXES, None),
    )
    return jax.shard_map(
        body,
        mesh=fine,
        in_specs=placed,
        out_specs=(P(AXES, None), P(AXES, None), P()),
        check_vma=False,
    )
```

time: 947 us -> 191 us (0.20)
  the two profiles are of different devices: /device:TPU:10 before, /device:TPU:2 now
where the time goes in v1:
time: 191 us; the launch traced here: 190 us
  blocking collectives  171 us (90%)
  Pallas kernels  8.21 us (4%)
  waiting for transfers between devices  4.61 us (2%)
  starting transfers between devices  3.83 us (2%)
    all_to_all x9, blocking collectives, exchange(): return lax.all_to_all(v, axis, 0, 0)  171 us
    pallas_call x9, Pallas kernels, call(): pl.pallas_call(kernel, out_shape=out_shapes, in_specs=in_specs, out_specs...  8.21 us
    ppermute x2, waiting for transfers between devices, swap(): return lax.ppermute(v, 'c', [(0, 1), (1, 0)])  4.61 us
    ppermute x2, starting transfers between devices, swap(): return lax.ppermute(v, 'c', [(0, 1), (1, 0)])  3.83 us
  transfers between devices with their start and end apart: 2, of which 2 were waited for; matrix products, arithmetic and copies ran while one was open for 0% of the time, Pallas kernels for 0%

profile of v1, /device:TPU:2, one launch (start us, length us, event | category | flops | bytes accessed | tf_op | source)
XLA Modules:
  0.0 189.8 jit_solution(12509746128199011030)
XLA Ops:
  0.6 0.9 broadcast_in_dim.6
  1.5 14.6 %all_to_all.45 = bf16[4,128,256]{2,1,0:T(8,128)(2,1)S(1)} all-to-all(bf16[4,128,256]{2,1,0:T(8,128)(2,1)S(1)} %broadcast_in_dim.6), channel_id=1, replica_groups=mesh['zl'=4,'y'=4,'c'=2,'x'=4,'zh'=4] {'zl'}, dimensions={0} | all-to-all | bytes 524288 | tf_op jit(solution)/shard_map/all_to_all | solution.py:168
  16.1 0.1 broadcast_in_dim.7
  16.1 0.0 copy-start
  16.1 0.0 copy-start.3
  16.2 0.0 copy-start.4
  16.2 17.2 %all_to_all.46 = bf16[4,512,256]{2,1,0:T(8,128)(2,1)S(1)} all-to-all(bf16[4,512,256]{2,1,0:T(8,128)(2,1)S(1)} %broadcast_in_dim.7), channel_id=1, replica_groups=mesh['zl'=4,'y'=4,'c'=2,'x'=4,'zh'=4] {'y'}, dimensions={0} | all-to-all | bytes 2097152 | tf_op jit(solution)/shard_map/all_to_all | solution.py:168
  33.3 1.9 %collective-permute-start = (bf16[16,128,256]{2,1,0:T(8,128)(2,1)S(1)}, bf16[16,128,256]{2,1,0:T(8,128)(2,1)S(1)}, u32[]{:S(2)}, u32[]{:S(2)}) collective-permute-start(bf16[16,128,256]{2,1,0:T(8,128)(2,1)S(1)} %bitcast.14), channel_id=1, source_target_pairs={{0,16},{16,0},{1,17},{17,1},{2,18},{18,2},{3,19},{19,3},{4,20},{20... | collective-permute-start | bytes 3145736 | tf_op jit(solution)/shard_map/ppermute | solution.py:172
  35.9 2.0 %collective-permute-done.other = bf16[16,128,256]{2,1,0:T(8,128)(2,1)S(1)} collective-permute-done((bf16[16,128,256]{2,1,0:T(8,128)(2,1)S(1)}, bf16[16,128,256]{2,1,0:T(8,128)(2,1)S(1)}, u32[]{:S(2)}, u32[]{:S(2)}) %collective-permute-start) | collective-permute-done | bytes 1048608 | tf_op jit(solution)/shard_map/ppermute | solution.py:172
  37.9 0.0 copy-done
  37.9 0.0 copy-done.3
  37.9 0.0 copy-done.4
  37.9 2.7 %shard_map.94 = bf16[16,128,256]{2,1,0:T(8,128)(2,1)S(1)} custom-call(s32[32]{0:T(128)S(1)} %bitcast.19, s32[32]{0:T(128)S(1)} %bitcast.21, s32[1]{0:T(128)} %bitcast.10.count, s32[1]{0:T(128)} %bitcast.3.me, bf16[32,128,128]{2,1,0:T(8,128)(2,1)S(1)} %bitcast.12, bf16[16,128,256]{2,1,0:T(8,128)(2,1)S(1)} %bitcast.15, ...), custom_call_target="tpu_custom_call" | custom-call | flops 268435456 | bytes 4194568 | tf_op jit(solution)/shard_map/pallas_call | solution.py:25
  40.6 17.8 %all_to_all.47.parts = bf16[4,512,256]{2,1,0:T(8,128)(2,1)S(1)} all-to-all(bf16[4,512,256]{2,1,0:T(8,128)(2,1)S(1)} %bitcast.16), channel_id=1, replica_groups=mesh['zl'=4,'y'=4,'c'=2,'x'=4,'zh'=4] {'x'}, dimensions={0} | all-to-all | bytes 2097152 | tf_op jit(solution)/shard_map/all_to_all | solution.py:168
  58.4 0.0 copy-start.1
  58.4 0.1 shard_map.95
  58.6 31.1 %all_to_all.48.parts = bf16[4,128,256]{2,1,0:T(8,128)(2,1)S(1)} all-to-all(bf16[4,128,256]{2,1,0:T(8,128)(2,1)S(1)} %bitcast.17), channel_id=1, replica_groups=mesh['zl'=4,'y'=4,'c'=2,'x'=4,'zh'=4] {'zh'}, dimensions={0} | all-to-all | bytes 524288 | tf_op jit(solution)/shard_map/all_to_all | solution.py:168
  89.7 0.0 copy-done.1
  89.7 0.0 copy-done.2
  89.7 0.9 shard_map.96
  90.5 14.7 %all_to_all.49.wparts = bf16[32,8,256]{2,1,0:T(8,128)(2,1)S(1)} all-to-all(bf16[32,8,256]{2,1,0:T(8,128)(2,1)S(1)} %bitcast.18), channel_id=1, replica_groups=mesh['zl'=4,'y'=4,'c'=2,'x'=4,'zh'=4] {'zl','y','c'}, dimensions={0} | all-to-all | bytes 262144 | tf_op jit(solution)/shard_map/all_to_all | solution.py:168
  105.3 24.0 %all_to_all.50.parts = bf16[4,144,256]{2,1,0:T(8,128)(2,1)S(1)} all-to-all(bf16[4,144,256]{2,1,0:T(8,128)(2,1)S(1)} %shard_map.97), channel_id=1, replica_groups=mesh['zl'=4,'y'=4,'c'=2,'x'=4,'zh'=4] {'zh'}, dimensions={0} | all-to-all | bytes 589824 | tf_op jit(solution)/shard_map/all_to_all | solution.py:168
  129.3 0.1 shard_map.98
  129.4 14.8 %all_to_all.51.cots = bf16[4,528,256]{2,1,0:T(8,128)(2,1)S(1)} all-to-all(bf16[4,528,256]{2,1,0:T(8,128)(2,1)S(1)} %shard_map.98), channel_id=1, replica_groups=mesh['zl'=4,'y'=4,'c'=2,'x'=4,'zh'=4] {'x'}, dimensions={0} | all-to-all | bytes 2162688 | tf_op jit(solution)/shard_map/all_to_all | solution.py:168
  144.2 3.2 %shard_map.99 = (bf16[2064,256]{1,0:T(8,128)(2,1)S(1)}, bf16[2064,256]{1,0:T(8,128)(2,1)S(1)}) custom-call(s32[32]{0:T(128)S(1)} %bitcast.20, s32[32]{0:T(128)S(1)} %bitcast.22, s32[1]{0:T(128)} %bitcast.11.count, s32[1]{0:T(128)} %bitcast.3.me, bf16[32,128,128]{2,1,0:T(8,128)(2,1)S(1)} %bitcast.13, bf16[4,528,256]{2,1,0:T(8,128)(2,1)S(1)} %all_to_all.51.cots), custom_call_target="tpu_custom_call" | custom-call | flops 268435456 | bytes 4243720 | tf_op jit(solution)/shard_map/pallas_call | solution.py:25
  147.4 1.9 %collective-permute-start.1 = (bf16[2064,256]{1,0:T(8,128)(2,1)S(1)}, bf16[2064,256]{1,0:T(8,128)(2,1)S(1)}, u32[]{:S(2)}, u32[]{:S(2)}) collective-permute-start(bf16[2064,256]{1,0:T(8,128)(2,1)S(1)} %get-tuple-element.14), channel_id=1, source_target_pairs={{0,16},{16,0},{1,17},{17,1},{2,18},{18,2},{3,19},{19,3},{4,20},{20... | collective-permute-start | bytes 3170312 | tf_op jit(solution)/shard_map/ppermute | solution.py:172
  149.3 2.6 %collective-permute-done.1.got = bf16[2064,256]{1,0:T(8,128)(2,1)S(1)} collective-permute-done((bf16[2064,256]{1,0:T(8,128)(2,1)S(1)}, bf16[2064,256]{1,0:T(8,128)(2,1)S(1)}, u32[]{:S(2)}, u32[]{:S(2)}) %collective-permute-start.1) | collective-permute-done | bytes 1056800 | tf_op jit(solution)/shard_map/ppermute | solution.py:172
  152.0 0.2 shard_map.100
  152.2 18.4 %all_to_all.52.parts = bf16[4,528,256]{2,1,0:T(8,128)(2,1)S(1)} all-to-all(bf16[4,528,256]{2,1,0:T(8,128)(2,1)S(1)} %shard_map.100), channel_id=1, replica_groups=mesh['zl'=4,'y'=4,'c'=2,'x'=4,'zh'=4] {'y'}, dimensions={0} | all-to-all | bytes 2162688 | tf_op jit(solution)/shard_map/all_to_all | solution.py:168
  170.7 0.1 shard_map.101
  170.8 18.2 %all_to_all.53.parts = bf16[4,192,256]{2,1,0:T(8,128)(2,1)S(1)} all-to-all(bf16[4,192,256]{2,1,0:T(8,128)(2,1)S(1)} %shard_map.101), channel_id=1, replica_groups=mesh['zl'=4,'y'=4,'c'=2,'x'=4,'zh'=4] {'zl'}, dimensions={0} | all-to-all | bytes 786432 | tf_op jit(solution)/shard_map/all_to_all | solution.py:168
  188.9 0.8 shard_map.102
  (2 shorter events, 0.0 us)
Async XLA Ops:
  16.1 21.7 %copy-start = (bf16[1,1,32,128,128]{4,3,2,1,0:T(8,128)(2,1)S(1)}, bf16[1,1,32,128,128]{4,3,2,1,0:T(8,128)(2,1)}, u32[]{:S(2)}) copy-start(bf16[1,1,32,128,128]{4,3,2,1,0:T(8,128)(2,1)} %param.8) | copy-start | bytes 3145732
  16.1 21.7 %copy-start.3 = (s32[1,1,32]{2,1,0:T(1,128)S(1)}, s32[1,1,32]{2,1,0:T(1,128)}, u32[]{:S(2)}) copy-start(s32[1,1,32]{2,1,0:T(1,128)} %param.9) | copy-start | bytes 388
  16.2 21.7 %copy-start.4 = (s32[1,1,32]{2,1,0:T(1,128)S(1)}, s32[1,1,32]{2,1,0:T(1,128)}, u32[]{:S(2)}) copy-start(s32[1,1,32]{2,1,0:T(1,128)} %param.10) | copy-start | bytes 388
  33.3 4.5 %collective-permute-start = (bf16[16,128,256]{2,1,0:T(8,128)(2,1)S(1)}, bf16[16,128,256]{2,1,0:T(8,128)(2,1)S(1)}, u32[]{:S(2)}, u32[]{:S(2)}) collective-permute-start(bf16[16,128,256]{2,1,0:T(8,128)(2,1)S(1)} %bitcast.14), channel_id=1, source_target_pairs={{0,16},{16,0},{1,17},{17,1},{2,18},{18,2},{3,19},{19,3},{4,20},{20... | collective-permute-start | bytes 3145736 | tf_op jit(solution)/shard_map/ppermute | solution.py:172
  58.4 31.2 %copy-start.1 = (bf16[256,256]{1,0:T(8,128)(2,1)S(1)}, bf16[256,256]{1,0:T(8,128)(2,1)}, u32[]{:S(2)}) copy-start(bf16[256,256]{1,0:T(8,128)(2,1)} %weight.3) | copy-start | bytes 393220
  58.4 31.2 %copy-start.2 = (bf16[128,256]{1,0:T(8,128)(2,1)S(1)}, bf16[128,256]{1,0:T(8,128)(2,1)}, u32[]{:S(2)}) copy-start(bf16[128,256]{1,0:T(8,128)(2,1)} %upstream.1) | copy-start | bytes 196612
  147.4 4.6 %collective-permute-start.1 = (bf16[2064,256]{1,0:T(8,128)(2,1)S(1)}, bf16[2064,256]{1,0:T(8,128)(2,1)S(1)}, u32[]{:S(2)}, u32[]{:S(2)}) collective-permute-start(bf16[2064,256]{1,0:T(8,128)(2,1)S(1)} %get-tuple-element.14), channel_id=1, source_target_pairs={{0,16},{16,0},{1,17},{17,1},{2,18},{18,2},{3,19},{19,3},{4,20},{20... | collective-permute-start | bytes 3170312 | tf_op jit(solution)/shard_map/ppermute | solution.py:172

commit v2 on v1

--- a/solution.py
+++ b/solution.py
@@ -48,11 +48,6 @@
     return terms[0]
 
 
-def split(v):
-    hi = v.astype(BF16)
-    return hi, (v - hi.astype(F32)).astype(BF16)
-
-
 def over_slots(count, step):
     def group(g, carry):
         for k in range(UNROLL):
@@ -97,17 +92,14 @@
 
 
 def pack_zh_kernel(wparts, cot, out):
-    hi, lo = split(total(wparts))
-    tail = jnp.concatenate([hi, lo], axis=0)
+    tail = total(wparts).astype(BF16)
     for d in range(4):
         out[d, :T] = cot[...]
         out[d, T:] = tail
 
 
 def pack_x_kernel(parts, out):
-    w = total(parts, slice(T, T + 16))
-    hi, lo = split(w[:8] + w[8:])
-    tail = jnp.concatenate([hi, lo], axis=0)
+    tail = total(parts, slice(T, T + 16)).astype(BF16)
     for d in range(4):
         for z in range(4):
             out[d, z * T : (z + 1) * T] = parts[z, :T]
@@ -131,21 +123,16 @@
     for k in range(16):
         own[k * T : (k + 1) * T] = acc[keep + k].astype(BF16)
         send[k * T : (k + 1) * T] = acc[give + k].astype(BF16)
-    w = total(cots, slice(4 * T, 4 * T + 16))
-    w = (w[:8] + w[8:]).astype(BF16)
-    w = jnp.concatenate([w, w], axis=0)
+    w = total(cots, slice(4 * T, 4 * T + 16)).astype(BF16)
     own[16 * T :] = w
     send[16 * T :] = w
 
 
-def pack_y_kernel(me, own, got, out):
+def pack_y_kernel(own, got, out):
     for y in range(4):
         block = slice(y * 4 * T, (y + 1) * 4 * T)
         out[y, : 4 * T] = (own[block].astype(F32) + got[block].astype(F32)).astype(BF16)
-    a = own[16 * T :].astype(F32)
-    b = got[16 * T :].astype(F32)
-    row = lax.broadcasted_iota(jnp.int32, (16, F), 0)
-    tail = jnp.where(row // 8 == me[0], a, b).astype(BF16)
+    tail = (own[16 * T :].astype(F32) + got[16 * T :].astype(F32)).astype(BF16)
     for y in range(4):
         out[y, 4 * T :] = tail
 
@@ -201,7 +188,7 @@
         (parts, weight, out_grad),
         8 * T * F * F,
     )
-    wparts = exchange(wterm.reshape(32, 8, F), ("zl", "y", "c"))
+    wparts = exchange(wterm.reshape(16, 16, F), ("zl", "y"))
 
     (packed,) = call(pack_zh_kernel, (sds(4, T + 16, F),), [VMEM] * 2, (wparts, cot), 2**20)
     parts = exchange(packed, "zh")
@@ -218,7 +205,7 @@
     )
     recv = swap(send)
     (packed,) = call(
-        pack_y_kernel, (sds(4, 4 * T + 16, F),), [SMEM] + [VMEM] * 2, (me, own, recv), 2**20
+        pack_y_kernel, (sds(4, 4 * T + 16, F),), [VMEM] * 2, (own, recv), 2**20
     )
     parts = exchange(packed, "y")
     (packed,) = call(pack_zl_kernel, (sds(4, T + 64, F),), [VMEM], (parts,), 2**20)

time: 191 us -> 183 us (0.958)
  the two profiles are of different devices: /device:TPU:2 before, /device:TPU:1 now
where the time goes in v2:
time: 183 us
  blocking collectives  155 us (85%)
  starting transfers between devices  13.7 us (7%)
  Pallas kernels  7.72 us (4%)
  waiting for transfers between devices  3.89 us (2%)
    all_to_all x9, blocking collectives, exchange(): return lax.all_to_all(v, axis, 0, 0)  155 us
    ppermute x2, starting transfers between devices, swap(): return lax.ppermute(v, 'c', [(0, 1), (1, 0)])  13.7 us
    pallas_call x9, Pallas kernels, call(): pl.pallas_call(kernel, out_shape=out_shapes, in_specs=in_specs, out_specs...  7.72 us
    ppermute x2, waiting for transfers between devices, swap(): return lax.ppermute(v, 'c', [(0, 1), (1, 0)])  3.89 us
  transfers between devices with their start and end apart: 2, of which 2 were waited for; matrix products, arithmetic and copies ran while one was open for 0% of the time, Pallas kernels for 0%

profile of v2, /device:TPU:1, one launch (start us, length us, event | category | flops | bytes accessed | tf_op | source)
XLA Modules:
  0.0 182.8 jit_solution(17802660220752301613)
XLA Ops:
  0.6 0.9 broadcast_in_dim.6
  1.5 12.2 %all_to_all.45 = bf16[4,128,256]{2,1,0:T(8,128)(2,1)S(1)} all-to-all(bf16[4,128,256]{2,1,0:T(8,128)(2,1)S(1)} %broadcast_in_dim.6), channel_id=1, replica_groups=mesh['zl'=4,'y'=4,'c'=2,'x'=4,'zh'=4] {'zl'}, dimensions={0} | all-to-all | bytes 524288 | tf_op jit(solution)/shard_map/all_to_all | solution.py:155
  13.7 0.1 broadcast_in_dim.7
  13.8 0.0 copy-start
  13.8 0.0 copy-start.3
  13.8 0.0 copy-start.4
  13.8 16.9 %all_to_all.46 = bf16[4,512,256]{2,1,0:T(8,128)(2,1)S(1)} all-to-all(bf16[4,512,256]{2,1,0:T(8,128)(2,1)S(1)} %broadcast_in_dim.7), channel_id=1, replica_groups=mesh['zl'=4,'y'=4,'c'=2,'x'=4,'zh'=4] {'y'}, dimensions={0} | all-to-all | bytes 2097152 | tf_op jit(solution)/shard_map/all_to_all | solution.py:155
  30.7 6.0 %collective-permute-start = (bf16[16,128,256]{2,1,0:T(8,128)(2,1)S(1)}, bf16[16,128,256]{2,1,0:T(8,128)(2,1)S(1)}, u32[]{:S(2)}, u32[]{:S(2)}) collective-permute-start(bf16[16,128,256]{2,1,0:T(8,128)(2,1)S(1)} %bitcast.14), channel_id=1, source_target_pairs={{0,16},{16,0},{1,17},{17,1},{2,18},{18,2},{3,19},{19,3},{4,20},{20... | collective-permute-start | bytes 3145736 | tf_op jit(solution)/shard_map/ppermute | solution.py:159
  37.4 1.6 collective-permute-done.other
  39.0 0.0 copy-done
  39.0 0.0 copy-done.3
  39.0 0.0 copy-done.4
  39.0 2.5 %shard_map.94 = bf16[16,128,256]{2,1,0:T(8,128)(2,1)S(1)} custom-call(s32[32]{0:T(128)S(1)} %bitcast.19, s32[32]{0:T(128)S(1)} %bitcast.21, s32[1]{0:T(128)} %bitcast.10.count, s32[1]{0:T(128)} %bitcast.3.me, bf16[32,128,128]{2,1,0:T(8,128)(2,1)S(1)} %bitcast.12, bf16[16,128,256]{2,1,0:T(8,128)(2,1)S(1)} %bitcast.15, ...), custom_call_target="tpu_custom_call" | custom-call | flops 268435456 | bytes 4194568 | tf_op jit(solution)/shard_map/pallas_call | solution.py:25
  41.5 18.9 %all_to_all.47.parts = bf16[4,512,256]{2,1,0:T(8,128)(2,1)S(1)} all-to-all(bf16[4,512,256]{2,1,0:T(8,128)(2,1)S(1)} %bitcast.16), channel_id=1, replica_groups=mesh['zl'=4,'y'=4,'c'=2,'x'=4,'zh'=4] {'x'}, dimensions={0} | all-to-all | bytes 2097152 | tf_op jit(solution)/shard_map/all_to_all | solution.py:155
  60.4 0.0 copy-start.1
  60.4 0.1 shard_map.95
  60.6 25.1 %all_to_all.48.parts = bf16[4,128,256]{2,1,0:T(8,128)(2,1)S(1)} all-to-all(bf16[4,128,256]{2,1,0:T(8,128)(2,1)S(1)} %bitcast.17), channel_id=1, replica_groups=mesh['zl'=4,'y'=4,'c'=2,'x'=4,'zh'=4] {'zh'}, dimensions={0} | all-to-all | bytes 524288 | tf_op jit(solution)/shard_map/all_to_all | solution.py:155
  85.7 0.0 copy-done.1
  85.7 0.0 copy-done.2
  85.7 0.9 shard_map.96
  86.6 18.3 %all_to_all.49.wparts = bf16[16,16,256]{2,1,0:T(8,128)(2,1)S(1)} all-to-all(bf16[16,16,256]{2,1,0:T(8,128)(2,1)S(1)} %bitcast.18), channel_id=1, replica_groups=mesh['zl'=4,'y'=4,'c'=2,'x'=4,'zh'=4] {'zl','y'}, dimensions={0} | all-to-all | bytes 262144 | tf_op jit(solution)/shard_map/all_to_all | solution.py:155
  104.9 19.8 %all_to_all.50.parts = bf16[4,144,256]{2,1,0:T(8,128)(2,1)S(1)} all-to-all(bf16[4,144,256]{2,1,0:T(8,128)(2,1)S(1)} %shard_map.97), channel_id=1, replica_groups=mesh['zl'=4,'y'=4,'c'=2,'x'=4,'zh'=4] {'zh'}, dimensions={0} | all-to-all | bytes 589824 | tf_op jit(solution)/shard_map/all_to_all | solution.py:155
  124.8 0.1 shard_map.98
  124.8 13.3 %all_to_all.51.cots = bf16[4,528,256]{2,1,0:T(8,128)(2,1)S(1)} all-to-all(bf16[4,528,256]{2,1,0:T(8,128)(2,1)S(1)} %shard_map.98), channel_id=1, replica_groups=mesh['zl'=4,'y'=4,'c'=2,'x'=4,'zh'=4] {'x'}, dimensions={0} | all-to-all | bytes 2162688 | tf_op jit(solution)/shard_map/all_to_all | solution.py:155
  138.1 2.9 %shard_map.99 = (bf16[2064,256]{1,0:T(8,128)(2,1)S(1)}, bf16[2064,256]{1,0:T(8,128)(2,1)S(1)}) custom-call(s32[32]{0:T(128)S(1)} %bitcast.20, s32[32]{0:T(128)S(1)} %bitcast.22, s32[1]{0:T(128)} %bitcast.11.count, s32[1]{0:T(128)} %bitcast.3.me, bf16[32,128,128]{2,1,0:T(8,128)(2,1)S(1)} %bitcast.13, bf16[4,528,256]{2,1,0:T(8,128)(2,1)S(1)} %all_to_all.51.cots), custom_call_target="tpu_custom_call" | custom-call | flops 268435456 | bytes 4243720 | tf_op jit(solution)/shard_map/pallas_call | solution.py:25
  141.1 7.7 %collective-permute-start.1 = (bf16[2064,256]{1,0:T(8,128)(2,1)S(1)}, bf16[2064,256]{1,0:T(8,128)(2,1)S(1)}, u32[]{:S(2)}, u32[]{:S(2)}) collective-permute-start(bf16[2064,256]{1,0:T(8,128)(2,1)S(1)} %get-tuple-element.14), channel_id=1, source_target_pairs={{0,16},{16,0},{1,17},{17,1},{2,18},{18,2},{3,19},{19,3},{4,20},{20... | collective-permute-start | bytes 3170312 | tf_op jit(solution)/shard_map/ppermute | solution.py:159
  148.7 2.3 %collective-permute-done.1.got = bf16[2064,256]{1,0:T(8,128)(2,1)S(1)} collective-permute-done((bf16[2064,256]{1,0:T(8,128)(2,1)S(1)}, bf16[2064,256]{1,0:T(8,128)(2,1)S(1)}, u32[]{:S(2)}, u32[]{:S(2)}) %collective-permute-start.1) | collective-permute-done | bytes 1056800 | tf_op jit(solution)/shard_map/ppermute | solution.py:159
  151.0 0.3 shard_map.100
  151.3 17.5 %all_to_all.52.parts = bf16[4,528,256]{2,1,0:T(8,128)(2,1)S(1)} all-to-all(bf16[4,528,256]{2,1,0:T(8,128)(2,1)S(1)} %shard_map.100), channel_id=1, replica_groups=mesh['zl'=4,'y'=4,'c'=2,'x'=4,'zh'=4] {'y'}, dimensions={0} | all-to-all | bytes 2162688 | tf_op jit(solution)/shard_map/all_to_all | solution.py:155
  168.8 0.1 shard_map.101
  168.9 13.1 %all_to_all.53.parts = bf16[4,192,256]{2,1,0:T(8,128)(2,1)S(1)} all-to-all(bf16[4,192,256]{2,1,0:T(8,128)(2,1)S(1)} %shard_map.101), channel_id=1, replica_groups=mesh['zl'=4,'y'=4,'c'=2,'x'=4,'zh'=4] {'zl'}, dimensions={0} | all-to-all | bytes 786432 | tf_op jit(solution)/shard_map/all_to_all | solution.py:155
  182.0 0.8 shard_map.102
  (2 shorter events, 0.0 us)
Async XLA Ops:
  13.8 25.2 %copy-start = (bf16[1,1,32,128,128]{4,3,2,1,0:T(8,128)(2,1)S(1)}, bf16[1,1,32,128,128]{4,3,2,1,0:T(8,128)(2,1)}, u32[]{:S(2)}) copy-start(bf16[1,1,32,128,128]{4,3,2,1,0:T(8,128)(2,1)} %param.8) | copy-start | bytes 3145732
  13.8 25.2 %copy-start.3 = (s32[1,1,32]{2,1,0:T(1,128)S(1)}, s32[1,1,32]{2,1,0:T(1,128)}, u32[]{:S(2)}) copy-start(s32[1,1,32]{2,1,0:T(1,128)} %param.9) | copy-start | bytes 388
  13.8 25.2 %copy-start.4 = (s32[1,1,32]{2,1,0:T(1,128)S(1)}, s32[1,1,32]{2,1,0:T(1,128)}, u32[]{:S(2)}) copy-start(s32[1,1,32]{2,1,0:T(1,128)} %param.10) | copy-start | bytes 388
  30.7 8.3 %collective-permute-start = (bf16[16,128,256]{2,1,0:T(8,128)(2,1)S(1)}, bf16[16,128,256]{2,1,0:T(8,128)(2,1)S(1)}, u32[]{:S(2)}, u32[]{:S(2)}) collective-permute-start(bf16[16,128,256]{2,1,0:T(8,128)(2,1)S(1)} %bitcast.14), channel_id=1, source_target_pairs={{0,16},{16,0},{1,17},{17,1},{2,18},{18,2},{3,19},{19,3},{4,20},{20... | collective-permute-start | bytes 3145736 | tf_op jit(solution)/shard_map/ppermute | solution.py:159
  60.4 25.3 %copy-start.1 = (bf16[256,256]{1,0:T(8,128)(2,1)S(1)}, bf16[256,256]{1,0:T(8,128)(2,1)}, u32[]{:S(2)}) copy-start(bf16[256,256]{1,0:T(8,128)(2,1)} %weight.3) | copy-start | bytes 393220
  60.4 25.3 %copy-start.2 = (bf16[128,256]{1,0:T(8,128)(2,1)S(1)}, bf16[128,256]{1,0:T(8,128)(2,1)}, u32[]{:S(2)}) copy-start(bf16[128,256]{1,0:T(8,128)(2,1)} %upstream.1) | copy-start | bytes 196612
  141.1 10.0 %collective-permute-start.1 = (bf16[2064,256]{1,0:T(8,128)(2,1)S(1)}, bf16[2064,256]{1,0:T(8,128)(2,1)S(1)}, u32[]{:S(2)}, u32[]{:S(2)}) collective-permute-start(bf16[2064,256]{1,0:T(8,128)(2,1)S(1)} %get-tuple-element.14), channel_id=1, source_target_pairs={{0,16},{16,0},{1,17},{17,1},{2,18},{18,2},{3,19},{19,3},{4,20},{20... | collective-permute-start | bytes 3170312 | tf_op jit(solution)/shard_map/ppermute | solution.py:159

commit v3 on v2

--- a/solution.py
+++ b/solution.py
@@ -14,6 +14,9 @@
 T = 128
 F = 256
 UNROLL = 4
+LAG_F = 3000
+LAG_B = 3000
+WHO = 0
 
 VMEM = pl.BlockSpec(memory_space=pltpu.VMEM)
 SMEM = pl.BlockSpec(memory_space=pltpu.SMEM)
@@ -62,6 +65,12 @@
     acc[...] = jnp.zeros_like(acc)
     mine = me[0]
 
+    if LAG_F:
+
+        @pl.when(mine == WHO)
+        def _():
+            pl.delay(LAG_F)
+
     def step(s, live):
         r, a = rows[s], cols[s]
         k = (a // 2) % 4 * 4 + a // 8
@@ -128,7 +137,13 @@
     send[16 * T :] = w
 
 
-def pack_y_kernel(own, got, out):
+def pack_y_kernel(me, own, got, out):
+    if LAG_B:
+
+        @pl.when(me[0] == WHO)
+        def _():
+            pl.delay(LAG_B)
+
     for y in range(4):
         block = slice(y * 4 * T, (y + 1) * 4 * T)
         out[y, : 4 * T] = (own[block].astype(F32) + got[block].astype(F32)).astype(BF16)
@@ -205,7 +220,7 @@
     )
     recv = swap(send)
     (packed,) = call(
-        pack_y_kernel, (sds(4, 4 * T + 16, F),), [VMEM] * 2, (own, recv), 2**20
+        pack_y_kernel, (sds(4, 4 * T + 16, F),), [SMEM] + [VMEM] * 2, (me, own, recv), 2**20
     )
     parts = exchange(packed, "y")
     (packed,) = call(pack_zl_kernel, (sds(4, T + 64, F),), [VMEM], (parts,), 2**20)

time: 183 us -> 175 us (0.956)
  the two profiles are of different devices: /device:TPU:1 before, /device:TPU:2 now
where the time goes in v3:
time: 175 us; the launch traced here: 174 us
  blocking collectives  151 us (86%)
  Pallas kernels  12.7 us (7%)
  waiting for transfers between devices  4.61 us (3%)
  starting transfers between devices  3.83 us (2%)
    all_to_all x9, blocking collectives, exchange(): return lax.all_to_all(v, axis, 0, 0)  151 us
    pallas_call x9, Pallas kernels, call(): pl.pallas_call(kernel, out_shape=out_shapes, in_specs=in_specs, out_specs...  12.7 us
    ppermute x2, waiting for transfers between devices, swap(): return lax.ppermute(v, 'c', [(0, 1), (1, 0)])  4.61 us
    ppermute x2, starting transfers between devices, swap(): return lax.ppermute(v, 'c', [(0, 1), (1, 0)])  3.83 us
  transfers between devices with their start and end apart: 2, of which 2 were waited for; matrix products, arithmetic and copies ran while one was open for 0% of the time, Pallas kernels for 0%

profile of v3, /device:TPU:2, one launch (start us, length us, event | category | flops | bytes accessed | tf_op | source)
XLA Modules:
  0.0 174.4 jit_solution(7025901365733248160)
XLA Ops:
  0.6 0.9 broadcast_in_dim.6
  1.5 14.6 %all_to_all.45 = bf16[4,128,256]{2,1,0:T(8,128)(2,1)S(1)} all-to-all(bf16[4,128,256]{2,1,0:T(8,128)(2,1)S(1)} %broadcast_in_dim.6), channel_id=1, replica_groups=mesh['zl'=4,'y'=4,'c'=2,'x'=4,'zh'=4] {'zl'}, dimensions={0} | all-to-all | bytes 524288 | tf_op jit(solution)/shard_map/all_to_all | solution.py:170
  16.1 0.1 broadcast_in_dim.7
  16.1 0.0 copy-start
  16.1 0.0 copy-start.3
  16.2 0.0 copy-start.4
  16.2 17.2 %all_to_all.46 = bf16[4,512,256]{2,1,0:T(8,128)(2,1)S(1)} all-to-all(bf16[4,512,256]{2,1,0:T(8,128)(2,1)S(1)} %broadcast_in_dim.7), channel_id=1, replica_groups=mesh['zl'=4,'y'=4,'c'=2,'x'=4,'zh'=4] {'y'}, dimensions={0} | all-to-all | bytes 2097152 | tf_op jit(solution)/shard_map/all_to_all | solution.py:170
  33.3 1.9 %collective-permute-start = (bf16[16,128,256]{2,1,0:T(8,128)(2,1)S(1)}, bf16[16,128,256]{2,1,0:T(8,128)(2,1)S(1)}, u32[]{:S(2)}, u32[]{:S(2)}) collective-permute-start(bf16[16,128,256]{2,1,0:T(8,128)(2,1)S(1)} %bitcast.14), channel_id=1, source_target_pairs={{0,16},{16,0},{1,17},{17,1},{2,18},{18,2},{3,19},{19,3},{4,20},{20... | collective-permute-start | bytes 3145736 | tf_op jit(solution)/shard_map/ppermute | solution.py:174
  35.9 2.0 %collective-permute-done.other = bf16[16,128,256]{2,1,0:T(8,128)(2,1)S(1)} collective-permute-done((bf16[16,128,256]{2,1,0:T(8,128)(2,1)S(1)}, bf16[16,128,256]{2,1,0:T(8,128)(2,1)S(1)}, u32[]{:S(2)}, u32[]{:S(2)}) %collective-permute-start) | collective-permute-done | bytes 1048608 | tf_op jit(solution)/shard_map/ppermute | solution.py:174
  37.9 0.0 copy-done
  37.9 0.0 copy-done.3
  37.9 0.0 copy-done.4
  37.9 5.0 %shard_map.94 = bf16[16,128,256]{2,1,0:T(8,128)(2,1)S(1)} custom-call(s32[32]{0:T(128)S(1)} %bitcast.19, s32[32]{0:T(128)S(1)} %bitcast.21, s32[1]{0:T(128)} %bitcast.10.count, s32[1]{0:T(128)} %bitcast.3.me, bf16[32,128,128]{2,1,0:T(8,128)(2,1)S(1)} %bitcast.12, bf16[16,128,256]{2,1,0:T(8,128)(2,1)S(1)} %bitcast.15, ...), custom_call_target="tpu_custom_call" | custom-call | flops 268435456 | bytes 4194568 | tf_op jit(solution)/shard_map/pallas_call | solution.py:28
  42.9 16.3 %all_to_all.47.parts = bf16[4,512,256]{2,1,0:T(8,128)(2,1)S(1)} all-to-all(bf16[4,512,256]{2,1,0:T(8,128)(2,1)S(1)} %bitcast.16), channel_id=1, replica_groups=mesh['zl'=4,'y'=4,'c'=2,'x'=4,'zh'=4] {'x'}, dimensions={0} | all-to-all | bytes 2097152 | tf_op jit(solution)/shard_map/all_to_all | solution.py:170
  59.2 0.0 copy-start.1
  59.2 0.1 shard_map.95
  59.3 28.1 %all_to_all.48.parts = bf16[4,128,256]{2,1,0:T(8,128)(2,1)S(1)} all-to-all(bf16[4,128,256]{2,1,0:T(8,128)(2,1)S(1)} %bitcast.17), channel_id=1, replica_groups=mesh['zl'=4,'y'=4,'c'=2,'x'=4,'zh'=4] {'zh'}, dimensions={0} | all-to-all | bytes 524288 | tf_op jit(solution)/shard_map/all_to_all | solution.py:170
  87.5 0.0 copy-done.1
  87.5 0.0 copy-done.2
  87.5 0.9 shard_map.96
  88.3 14.9 %all_to_all.49.wparts = bf16[16,16,256]{2,1,0:T(8,128)(2,1)S(1)} all-to-all(bf16[16,16,256]{2,1,0:T(8,128)(2,1)S(1)} %bitcast.18), channel_id=1, replica_groups=mesh['zl'=4,'y'=4,'c'=2,'x'=4,'zh'=4] {'zl','y'}, dimensions={0} | all-to-all | bytes 262144 | tf_op jit(solution)/shard_map/all_to_all | solution.py:170
  103.3 17.9 %all_to_all.50.parts = bf16[4,144,256]{2,1,0:T(8,128)(2,1)S(1)} all-to-all(bf16[4,144,256]{2,1,0:T(8,128)(2,1)S(1)} %shard_map.97), channel_id=1, replica_groups=mesh['zl'=4,'y'=4,'c'=2,'x'=4,'zh'=4] {'zh'}, dimensions={0} | all-to-all | bytes 589824 | tf_op jit(solution)/shard_map/all_to_all | solution.py:170
  121.2 0.1 shard_map.98
  121.2 13.5 %all_to_all.51.cots = bf16[4,528,256]{2,1,0:T(8,128)(2,1)S(1)} all-to-all(bf16[4,528,256]{2,1,0:T(8,128)(2,1)S(1)} %shard_map.98), channel_id=1, replica_groups=mesh['zl'=4,'y'=4,'c'=2,'x'=4,'zh'=4] {'x'}, dimensions={0} | all-to-all | bytes 2162688 | tf_op jit(solution)/shard_map/all_to_all | solution.py:170
  134.7 2.4 %shard_map.99 = (bf16[2064,256]{1,0:T(8,128)(2,1)S(1)}, bf16[2064,256]{1,0:T(8,128)(2,1)S(1)}) custom-call(s32[32]{0:T(128)S(1)} %bitcast.20, s32[32]{0:T(128)S(1)} %bitcast.22, s32[1]{0:T(128)} %bitcast.11.count, s32[1]{0:T(128)} %bitcast.3.me, bf16[32,128,128]{2,1,0:T(8,128)(2,1)S(1)} %bitcast.13, bf16[4,528,256]{2,1,0:T(8,128)(2,1)S(1)} %all_to_all.51.cots), custom_call_target="tpu_custom_call" | custom-call | flops 268435456 | bytes 4243720 | tf_op jit(solution)/shard_map/pallas_call | solution.py:28
  137.1 1.9 %collective-permute-start.1 = (bf16[2064,256]{1,0:T(8,128)(2,1)S(1)}, bf16[2064,256]{1,0:T(8,128)(2,1)S(1)}, u32[]{:S(2)}, u32[]{:S(2)}) collective-permute-start(bf16[2064,256]{1,0:T(8,128)(2,1)S(1)} %get-tuple-element.14), channel_id=1, source_target_pairs={{0,16},{16,0},{1,17},{17,1},{2,18},{18,2},{3,19},{19,3},{4,20},{20... | collective-permute-start | bytes 3170312 | tf_op jit(solution)/shard_map/ppermute | solution.py:174
  139.0 2.6 %collective-permute-done.1.got = bf16[2064,256]{1,0:T(8,128)(2,1)S(1)} collective-permute-done((bf16[2064,256]{1,0:T(8,128)(2,1)S(1)}, bf16[2064,256]{1,0:T(8,128)(2,1)S(1)}, u32[]{:S(2)}, u32[]{:S(2)}) %collective-permute-start.1) | collective-permute-done | bytes 1056800 | tf_op jit(solution)/shard_map/ppermute | solution.py:174
  141.6 3.2 %shard_map.100 = bf16[4,528,256]{2,1,0:T(8,128)(2,1)S(1)} custom-call(s32[1]{0:T(128)} %bitcast.3.me, bf16[2064,256]{1,0:T(8,128)(2,1)S(1)} %get-tuple-element.13.own, bf16[2064,256]{1,0:T(8,128)(2,1)S(1)} %collective-permute-done.1.got), custom_call_target="tpu_custom_call" | custom-call | flops 1048576 | bytes 3194884 | tf_op jit(solution)/shard_map/pallas_call | solution.py:28
  144.9 15.4 %all_to_all.52.parts = bf16[4,528,256]{2,1,0:T(8,128)(2,1)S(1)} all-to-all(bf16[4,528,256]{2,1,0:T(8,128)(2,1)S(1)} %shard_map.100), channel_id=1, replica_groups=mesh['zl'=4,'y'=4,'c'=2,'x'=4,'zh'=4] {'y'}, dimensions={0} | all-to-all | bytes 2162688 | tf_op jit(solution)/shard_map/all_to_all | solution.py:170
  160.3 0.1 shard_map.101
  160.4 13.2 %all_to_all.53.parts = bf16[4,192,256]{2,1,0:T(8,128)(2,1)S(1)} all-to-all(bf16[4,192,256]{2,1,0:T(8,128)(2,1)S(1)} %shard_map.101), channel_id=1, replica_groups=mesh['zl'=4,'y'=4,'c'=2,'x'=4,'zh'=4] {'zl'}, dimensions={0} | all-to-all | bytes 786432 | tf_op jit(solution)/shard_map/all_to_all | solution.py:170
  173.6 0.8 shard_map.102
  (2 shorter events, 0.0 us)
Async XLA Ops:
  16.1 21.7 %copy-start = (bf16[1,1,32,128,128]{4,3,2,1,0:T(8,128)(2,1)S(1)}, bf16[1,1,32,128,128]{4,3,2,1,0:T(8,128)(2,1)}, u32[]{:S(2)}) copy-start(bf16[1,1,32,128,128]{4,3,2,1,0:T(8,128)(2,1)} %param.8) | copy-start | bytes 3145732
  16.1 21.7 %copy-start.3 = (s32[1,1,32]{2,1,0:T(1,128)S(1)}, s32[1,1,32]{2,1,0:T(1,128)}, u32[]{:S(2)}) copy-start(s32[1,1,32]{2,1,0:T(1,128)} %param.9) | copy-start | bytes 388
  16.2 21.7 %copy-start.4 = (s32[1,1,32]{2,1,0:T(1,128)S(1)}, s32[1,1,32]{2,1,0:T(1,128)}, u32[]{:S(2)}) copy-start(s32[1,1,32]{2,1,0:T(1,128)} %param.10) | copy-start | bytes 388
  33.3 4.5 %collective-permute-start = (bf16[16,128,256]{2,1,0:T(8,128)(2,1)S(1)}, bf16[16,128,256]{2,1,0:T(8,128)(2,1)S(1)}, u32[]{:S(2)}, u32[]{:S(2)}) collective-permute-start(bf16[16,128,256]{2,1,0:T(8,128)(2,1)S(1)} %bitcast.14), channel_id=1, source_target_pairs={{0,16},{16,0},{1,17},{17,1},{2,18},{18,2},{3,19},{19,3},{4,20},{20... | collective-permute-start | bytes 3145736 | tf_op jit(solution)/shard_map/ppermute | solution.py:174
  59.2 28.3 %copy-start.1 = (bf16[256,256]{1,0:T(8,128)(2,1)S(1)}, bf16[256,256]{1,0:T(8,128)(2,1)}, u32[]{:S(2)}) copy-start(bf16[256,256]{1,0:T(8,128)(2,1)} %weight.3) | copy-start | bytes 393220
  59.2 28.3 %copy-start.2 = (bf16[128,256]{1,0:T(8,128)(2,1)S(1)}, bf16[128,256]{1,0:T(8,128)(2,1)}, u32[]{:S(2)}) copy-start(bf16[128,256]{1,0:T(8,128)(2,1)} %upstream.1) | copy-start | bytes 196612
  137.1 4.6 %collective-permute-start.1 = (bf16[2064,256]{1,0:T(8,128)(2,1)S(1)}, bf16[2064,256]{1,0:T(8,128)(2,1)S(1)}, u32[]{:S(2)}, u32[]{:S(2)}) collective-permute-start(bf16[2064,256]{1,0:T(8,128)(2,1)S(1)} %get-tuple-element.14), channel_id=1, source_target_pairs={{0,16},{16,0},{1,17},{17,1},{2,18},{18,2},{3,19},{19,3},{4,20},{20... | collective-permute-start | bytes 3170312 | tf_op jit(solution)/shard_map/ppermute | solution.py:174

commit v4 on v2

--- a/solution.py
+++ b/solution.py
@@ -14,19 +14,22 @@
 T = 128
 F = 256
 UNROLL = 4
+LAG_F = 3000
+LAG_B = 3000
 
 VMEM = pl.BlockSpec(memory_space=pltpu.VMEM)
 SMEM = pl.BlockSpec(memory_space=pltpu.SMEM)
 
 
-def call(kernel, out_shapes, in_specs, args, flops, scratch=()):
+def call(kernel, out_shapes, in_specs, args, flops, scratch=(), out_specs=None, aliases={}):
     nbytes = sum(a.size * a.dtype.itemsize for a in args)
     nbytes += sum(s.size * s.dtype.itemsize for s in out_shapes)
     return pl.pallas_call(
         kernel,
         out_shape=out_shapes,
         in_specs=in_specs,
-        out_specs=tuple(VMEM for _ in out_shapes),
+        out_specs=out_specs or tuple(VMEM for _ in out_shapes),
+        input_output_aliases=aliases,
         scratch_shapes=list(scratch),
         compiler_params=pltpu.CompilerParams(vmem_limit_bytes=24 * 2**20),
         cost_estimate=pl.CostEstimate(flops=flops, bytes_accessed=nbytes, transcendentals=0),
@@ -39,6 +42,12 @@
 
 def dot(a, b, da, db):
     return lax.dot_general(a, b, (((da,), (db,)), ((), ())), preferred_element_type=F32)
+
+
+def lag(me, amount):
+    @pl.when(me[0] == 0)
+    def _():
+        pl.delay(amount)
 
 
 def total(ref, *index):
@@ -48,28 +57,48 @@
     return terms[0]
 
 
-def over_slots(count, step):
+def half_index(col_tile):
+    return (col_tile // 2) % 4 * 4 + col_tile // 8
+
+
+def over_slots(count, near, order, step):
     def group(g, carry):
         for k in range(UNROLL):
-            s = g * UNROLL + k
-            step(s, s < count)
+            i = g * UNROLL + k
+            step(order[31 - i if near else i], i < count)
         return carry
 
     lax.fori_loop(0, (count + UNROLL - 1) // UNROLL, group, 0)
 
 
-def forward_kernel(rows, cols, count, me, tiles, own, other, out, acc):
+def near_kernel(rows, cols, count, me, tiles, own, acc, order, far):
     acc[...] = jnp.zeros_like(acc)
     mine = me[0]
+    for i in range(32):
+        order[i] = 0
+
+    def place(s, n_far):
+        is_far = (cols[s] % 2 != mine).astype(jnp.int32)
+        order[jnp.where(is_far == 1, n_far, 31 - (s - n_far))] = s
+        return n_far + is_far
+
+    n_far = lax.fori_loop(0, count[0], place, jnp.int32(0))
+    far[0] = n_far
 
     def step(s, live):
-        r, a = rows[s], cols[s]
-        k = (a // 2) % 4 * 4 + a // 8
-        source = jnp.where(a % 2 == mine, own[k], other[k])
         tile = jnp.where(live, tiles[s], jnp.zeros((), BF16))
-        acc[r] += dot(tile, source, 1, 0)
-
-    over_slots(count[0], step)
+        acc[rows[s]] += dot(tile, own[half_index(cols[s])], 1, 0)
+
+    over_slots(count[0] - n_far, True, order, step)
+
+
+def far_kernel(rows, cols, me, order, far, tiles, other, given, out, acc):
+    def step(s, live):
+        tile = jnp.where(live, tiles[s], jnp.zeros((), BF16))
+        acc[rows[s]] += dot(tile, other[half_index(cols[s])], 1, 0)
+
+    over_slots(far[0], False, order, step)
+    lag(me, LAG_F)
     out[...] = acc[...].astype(BF16)
 
 
@@ -106,29 +135,23 @@
         out[d, 4 * T :] = tail
 
 
-def backward_kernel(rows, cols, count, me, tiles, cots, own, send, acc):
+def backward_kernel(near, rows, cols, count, order, far, tiles, cots, out, acc):
     acc[...] = jnp.zeros_like(acc)
-    mine = me[0]
 
     def step(s, live):
-        r, a = rows[s], cols[s]
-        k = a % 2 * 16 + (a // 2) % 4 * 4 + a // 8
+        r = rows[s]
         source = cots[r // 4, pl.ds(pl.multiple_of(r % 4 * T, T), T)]
         tile = jnp.where(live, tiles[s], jnp.zeros((), BF16))
-        acc[k] += dot(tile, source, 0, 0)
-
-    over_slots(count[0], step)
-    keep = mine * 16
-    give = 16 - keep
+        acc[half_index(cols[s])] += dot(tile, source, 0, 0)
+
+    over_slots(count[0] - far[0] if near else far[0], near, order, step)
     for k in range(16):
-        own[k * T : (k + 1) * T] = acc[keep + k].astype(BF16)
-        send[k * T : (k + 1) * T] = acc[give + k].astype(BF16)
-    w = total(cots, slice(4 * T, 4 * T + 16)).astype(BF16)
-    own[16 * T :] = w
-    send[16 * T :] = w
-
-
-def pack_y_kernel(own, got, out):
+        out[k * T : (k + 1) * T] = acc[k].astype(BF16)
+    out[16 * T :] = total(cots, slice(4 * T, 4 * T + 16)).astype(BF16)
+
+
+def pack_y_kernel(me, own, got, out):
+    lag(me, LAG_B)
     for y in range(4):
         block = slice(y * 4 * T, (y + 1) * 4 * T)
         out[y, : 4 * T] = (own[block].astype(F32) + got[block].astype(F32)).astype(BF16)
@@ -169,14 +192,21 @@
     got = exchange(jnp.broadcast_to(features, (4, T, F)), "zl").reshape(4 * T, F)
     got = exchange(jnp.broadcast_to(got, (4, 4 * T, F)), "y").reshape(16, T, F)
     other = swap(got)
-
-    (partial,) = call(
-        forward_kernel,
-        (sds(16, T, F),),
-        [SMEM] * 4 + [VMEM] * 3,
-        (rows, cols, count, me, tiles, got, other),
+    acc, order, far = call(
+        near_kernel,
+        (sds(16, T, F, dtype=F32), sds(32, dtype=jnp.int32), sds(1, dtype=jnp.int32)),
+        [SMEM] * 4 + [VMEM] * 2,
+        (rows, cols, count, me, tiles, got),
         tile_flops,
-        [pltpu.VMEM((16, T, F), F32)],
+        out_specs=(VMEM, SMEM, SMEM),
+    )
+    partial, _ = call(
+        far_kernel,
+        (sds(16, T, F), sds(16, T, F, dtype=F32)),
+        [SMEM] * 5 + [VMEM] * 3,
+        (rows, cols, me, order, far, tiles, other, acc),
+        tile_flops,
+        aliases={7: 1},
     )
     parts = exchange(partial.reshape(4, 4 * T, F), "x")
     (summed,) = call(sum_kernel, (sds(4 * T, F),), [VMEM], (parts,), 2**20)
@@ -195,17 +225,20 @@
     (packed,) = call(pack_x_kernel, (sds(4, 4 * T + 16, F),), [VMEM], (parts,), 2**20)
     cots = exchange(packed, "x")
 
-    own, send = call(
-        backward_kernel,
-        (sds(16 * T + 16, F), sds(16 * T + 16, F)),
-        [SMEM] * 4 + [VMEM] * 2,
-        (rows, cols, count, me, tiles, cots),
-        tile_flops,
-        [pltpu.VMEM((32, T, F), F32)],
+    send, own = (
+        call(
+            functools.partial(backward_kernel, near),
+            (sds(16 * T + 16, F),),
+            [SMEM] * 5 + [VMEM] * 2,
+            (rows, cols, count, order, far, tiles, cots),
+            tile_flops,
+            [pltpu.VMEM((16, T, F), F32)],
+        )[0]
+        for near in (False, True)
     )
     recv = swap(send)
     (packed,) = call(
-        pack_y_kernel, (sds(4, 4 * T + 16, F),), [VMEM] * 2, (own, recv), 2**20
+        pack_y_kernel, (sds(4, 4 * T + 16, F),), [SMEM] + [VMEM] * 2, (me, own, recv), 2**20
     )
     parts = exchange(packed, "y")
     (packed,) = call(pack_zl_kernel, (sds(4, T + 64, F),), [VMEM], (parts,), 2**20)

time: 183 us -> 177 us (0.967)
  the two profiles are of different devices: /device:TPU:1 before, /device:TPU:2 now
where the time goes in v4:
time: 177 us; the launch traced here: 176 us
  blocking collectives  151 us (85%)
  Pallas kernels  18.3 us (10%)
  starting transfers between devices  3.83 us (2%)
    all_to_all x9, blocking collectives, exchange(): return lax.all_to_all(v, axis, 0, 0)  151 us
    pallas_call x11, Pallas kernels, call(): pl.pallas_call(kernel, out_shape=out_shapes, in_specs=in_specs, out_specs...  18.3 us
    ppermute x2, starting transfers between devices, swap(): return lax.ppermute(v, 'c', [(0, 1), (1, 0)])  3.83 us
  transfers between devices with their start and end apart: 2, of which 1 were waited for; matrix products, arithmetic and copies ran while one was open for 0% of the time, Pallas kernels for 3%

profile of v4, /device:TPU:2, one launch (start us, length us, event | category | flops | bytes accessed | tf_op | source)
XLA Modules:
  0.0 175.9 jit_solution(4286172136458770282)
XLA Ops:
  0.6 0.9 broadcast_in_dim.6
  1.5 14.6 %all_to_all.45 = bf16[4,128,256]{2,1,0:T(8,128)(2,1)S(1)} all-to-all(bf16[4,128,256]{2,1,0:T(8,128)(2,1)S(1)} %broadcast_in_dim.6), channel_id=1, replica_groups=mesh['zl'=4,'y'=4,'c'=2,'x'=4,'zh'=4] {'zl'}, dimensions={0} | all-to-all | bytes 524288 | tf_op jit(solution)/shard_map/all_to_all | solution.py:178
  16.1 0.1 broadcast_in_dim.7
  16.1 0.0 copy-start
  16.1 0.0 copy-start.3
  16.2 0.0 copy-start.4
  16.2 17.2 %all_to_all.46 = bf16[4,512,256]{2,1,0:T(8,128)(2,1)S(1)} all-to-all(bf16[4,512,256]{2,1,0:T(8,128)(2,1)S(1)} %broadcast_in_dim.7), channel_id=1, replica_groups=mesh['zl'=4,'y'=4,'c'=2,'x'=4,'zh'=4] {'y'}, dimensions={0} | all-to-all | bytes 2097152 | tf_op jit(solution)/shard_map/all_to_all | solution.py:178
  33.3 1.9 %collective-permute-start = (bf16[16,128,256]{2,1,0:T(8,128)(2,1)S(1)}, bf16[16,128,256]{2,1,0:T(8,128)(2,1)S(1)}, u32[]{:S(2)}, u32[]{:S(2)}) collective-permute-start(bf16[16,128,256]{2,1,0:T(8,128)(2,1)S(1)} %bitcast.17), channel_id=1, source_target_pairs={{0,16},{16,0},{1,17},{17,1},{2,18},{18,2},{3,19},{19,3},{4,20},{20... | collective-permute-start | bytes 3145736 | tf_op jit(solution)/shard_map/ppermute | solution.py:182
  35.9 0.0 copy-done
  35.9 0.0 copy-done.3
  35.9 0.0 copy-done.4
  35.9 2.7 %shard_map.94 = (f32[16,128,256]{2,1,0:T(8,128)S(1)}, s32[32]{0:T(128)S(1)}, s32[1]{0:T(128)}) custom-call(s32[32]{0:T(128)S(1)} %bitcast.22, s32[32]{0:T(128)S(1)} %bitcast.26, s32[1]{0:T(128)} %bitcast.10.count, s32[1]{0:T(128)} %bitcast.2.me, bf16[32,128,128]{2,1,0:T(8,128)(2,1)S(1)} %bitcast.13, bf16[16,128,256]{2,1,0:T(8,128)(2,1)S(1)} %bitcast.18), custom_call_target="tpu_custom_call" | custom-call | flops 268435456 | bytes 4194700 | tf_op jit(solution)/shard_map/pallas_call | solution.py:27
  38.6 0.0 collective-permute-done.other
  38.6 5.3 %shard_map.95 = (bf16[16,128,256]{2,1,0:T(8,128)(2,1)S(1)}, f32[16,128,256]{2,1,0:T(8,128)S(1)}) custom-call(s32[32]{0:T(128)S(1)} %bitcast.23, s32[32]{0:T(128)S(1)} %bitcast.27, s32[1]{0:T(128)} %bitcast.2.me, s32[32]{0:T(128)S(1)} %get-tuple-element.12.order, s32[1]{0:T(128)} %get-tuple-element.13.far, ...), custom_call_target="tpu_custom_call", output_to_operand_aliasing={{1}: (7, {})} | custom-call | flops 268435456 | bytes 7340424 | tf_op jit(solution)/shard_map/pallas_call | solution.py:27
  43.9 15.3 %all_to_all.47.parts = bf16[4,512,256]{2,1,0:T(8,128)(2,1)S(1)} all-to-all(bf16[4,512,256]{2,1,0:T(8,128)(2,1)S(1)} %bitcast.20), channel_id=1, replica_groups=mesh['zl'=4,'y'=4,'c'=2,'x'=4,'zh'=4] {'x'}, dimensions={0} | all-to-all | bytes 2097152 | tf_op jit(solution)/shard_map/all_to_all | solution.py:178
  59.2 0.1 shard_map.96
  59.4 28.7 %all_to_all.48.parts = bf16[4,128,256]{2,1,0:T(8,128)(2,1)S(1)} all-to-all(bf16[4,128,256]{2,1,0:T(8,128)(2,1)S(1)} %bitcast.19), channel_id=1, replica_groups=mesh['zl'=4,'y'=4,'c'=2,'x'=4,'zh'=4] {'zh'}, dimensions={0} | all-to-all | bytes 524288 | tf_op jit(solution)/shard_map/all_to_all | solution.py:178
  88.0 0.0 copy-done.1
  88.0 0.9 shard_map.97
  88.9 14.1 %all_to_all.49.wparts = bf16[16,16,256]{2,1,0:T(8,128)(2,1)S(1)} all-to-all(bf16[16,16,256]{2,1,0:T(8,128)(2,1)S(1)} %bitcast.21), channel_id=1, replica_groups=mesh['zl'=4,'y'=4,'c'=2,'x'=4,'zh'=4] {'zl','y'}, dimensions={0} | all-to-all | bytes 262144 | tf_op jit(solution)/shard_map/all_to_all | solution.py:178
  103.0 17.8 %all_to_all.50.parts = bf16[4,144,256]{2,1,0:T(8,128)(2,1)S(1)} all-to-all(bf16[4,144,256]{2,1,0:T(8,128)(2,1)S(1)} %shard_map.98), channel_id=1, replica_groups=mesh['zl'=4,'y'=4,'c'=2,'x'=4,'zh'=4] {'zh'}, dimensions={0} | all-to-all | bytes 589824 | tf_op jit(solution)/shard_map/all_to_all | solution.py:178
  120.8 0.1 shard_map.99
  120.9 14.6 %all_to_all.51.cots = bf16[4,528,256]{2,1,0:T(8,128)(2,1)S(1)} all-to-all(bf16[4,528,256]{2,1,0:T(8,128)(2,1)S(1)} %shard_map.99), channel_id=1, replica_groups=mesh['zl'=4,'y'=4,'c'=2,'x'=4,'zh'=4] {'x'}, dimensions={0} | all-to-all | bytes 2162688 | tf_op jit(solution)/shard_map/all_to_all | solution.py:178
  135.5 2.5 %shard_map.101 = bf16[2064,256]{1,0:T(8,128)(2,1)S(1)} custom-call(s32[32]{0:T(128)S(1)} %bitcast.24, s32[32]{0:T(128)S(1)} %bitcast.28, s32[1]{0:T(128)} %bitcast.12.count, s32[32]{0:T(128)S(1)} %get-tuple-element.12.order, s32[1]{0:T(128)} %get-tuple-element.13.far, bf16[32,128,128]{2,1,0:T(8,128)(2,1)S(1)} %bitcast.15, ...), custom_call_target="tpu_custom_call" | custom-call | flops 268435456 | bytes 3187080 | tf_op jit(solution)/shard_map/pallas_call | solution.py:27
  138.0 1.9 %collective-permute-start.1 = (bf16[2064,256]{1,0:T(8,128)(2,1)S(1)}, bf16[2064,256]{1,0:T(8,128)(2,1)S(1)}, u32[]{:S(2)}, u32[]{:S(2)}) collective-permute-start(bf16[2064,256]{1,0:T(8,128)(2,1)S(1)} %shard_map.101), channel_id=1, source_target_pairs={{0,16},{16,0},{1,17},{17,1},{2,18},{18,2},{3,19},{19,3},{4,20},{20... | collective-permute-start | bytes 3170312 | tf_op jit(solution)/shard_map/ppermute | solution.py:182
  139.9 2.5 %shard_map.100.own = bf16[2064,256]{1,0:T(8,128)(2,1)S(1)} custom-call(s32[32]{0:T(128)S(1)} %bitcast.25, s32[32]{0:T(128)S(1)} %bitcast.29, s32[1]{0:T(128)} %bitcast.11.count, s32[32]{0:T(128)S(1)} %get-tuple-element.12.order, s32[1]{0:T(128)} %get-tuple-element.13.far, bf16[32,128,128]{2,1,0:T(8,128)(2,1)S(1)} %bitcast.16, ...), custom_call_target="tpu_custom_call" | custom-call | flops 268435456 | bytes 3187080 | tf_op jit(solution)/shard_map/pallas_call | solution.py:27
  142.4 0.1 collective-permute-done.1.got
  142.5 3.2 %shard_map.102 = bf16[4,528,256]{2,1,0:T(8,128)(2,1)S(1)} custom-call(s32[1]{0:T(128)} %bitcast.2.me, bf16[2064,256]{1,0:T(8,128)(2,1)S(1)} %shard_map.100.own, bf16[2064,256]{1,0:T(8,128)(2,1)S(1)} %collective-permute-done.1.got), custom_call_target="tpu_custom_call" | custom-call | flops 1048576 | bytes 3194884 | tf_op jit(solution)/shard_map/pallas_call | solution.py:27
  145.8 16.4 %all_to_all.52.parts = bf16[4,528,256]{2,1,0:T(8,128)(2,1)S(1)} all-to-all(bf16[4,528,256]{2,1,0:T(8,128)(2,1)S(1)} %shard_map.102), channel_id=1, replica_groups=mesh['zl'=4,'y'=4,'c'=2,'x'=4,'zh'=4] {'y'}, dimensions={0} | all-to-all | bytes 2162688 | tf_op jit(solution)/shard_map/all_to_all | solution.py:178
  162.2 0.1 shard_map.103
  162.3 12.7 %all_to_all.53.parts = bf16[4,192,256]{2,1,0:T(8,128)(2,1)S(1)} all-to-all(bf16[4,192,256]{2,1,0:T(8,128)(2,1)S(1)} %shard_map.103), channel_id=1, replica_groups=mesh['zl'=4,'y'=4,'c'=2,'x'=4,'zh'=4] {'zl'}, dimensions={0} | all-to-all | bytes 786432 | tf_op jit(solution)/shard_map/all_to_all | solution.py:178
  175.0 0.8 shard_map.104
  (4 shorter events, 0.0 us)
Async XLA Ops:
  16.1 19.8 %copy-start = (bf16[1,1,32,128,128]{4,3,2,1,0:T(8,128)(2,1)S(1)}, bf16[1,1,32,128,128]{4,3,2,1,0:T(8,128)(2,1)}, u32[]{:S(2)}) copy-start(bf16[1,1,32,128,128]{4,3,2,1,0:T(8,128)(2,1)} %param.8) | copy-start | bytes 3145732
  16.1 19.8 %copy-start.3 = (s32[1,1,32]{2,1,0:T(1,128)S(1)}, s32[1,1,32]{2,1,0:T(1,128)}, u32[]{:S(2)}) copy-start(s32[1,1,32]{2,1,0:T(1,128)} %param.9) | copy-start | bytes 388
  16.2 19.8 %copy-start.4 = (s32[1,1,32]{2,1,0:T(1,128)S(1)}, s32[1,1,32]{2,1,0:T(1,128)}, u32[]{:S(2)}) copy-start(s32[1,1,32]{2,1,0:T(1,128)} %param.10) | copy-start | bytes 388
  33.3 5.3 %collective-permute-start = (bf16[16,128,256]{2,1,0:T(8,128)(2,1)S(1)}, bf16[16,128,256]{2,1,0:T(8,128)(2,1)S(1)}, u32[]{:S(2)}, u32[]{:S(2)}) collective-permute-start(bf16[16,128,256]{2,1,0:T(8,128)(2,1)S(1)} %bitcast.17), channel_id=1, source_target_pairs={{0,16},{16,0},{1,17},{17,1},{2,18},{18,2},{3,19},{19,3},{4,20},{20... | collective-permute-start | bytes 3145736 | tf_op jit(solution)/shard_map/ppermute | solution.py:182
  59.2 28.8 %copy-start.1 = (bf16[256,256]{1,0:T(8,128)(2,1)S(1)}, bf16[256,256]{1,0:T(8,128)(2,1)}, u32[]{:S(2)}) copy-start(bf16[256,256]{1,0:T(8,128)(2,1)} %weight.3) | copy-start | bytes 393220
  59.2 28.8 %copy-start.2 = (bf16[128,256]{1,0:T(8,128)(2,1)S(1)}, bf16[128,256]{1,0:T(8,128)(2,1)}, u32[]{:S(2)}) copy-start(bf16[128,256]{1,0:T(8,128)(2,1)} %upstream.1) | copy-start | bytes 196612
  138.0 4.6 %collective-permute-start.1 = (bf16[2064,256]{1,0:T(8,128)(2,1)S(1)}, bf16[2064,256]{1,0:T(8,128)(2,1)S(1)}, u32[]{:S(2)}, u32[]{:S(2)}) collective-permute-start(bf16[2064,256]{1,0:T(8,128)(2,1)S(1)} %shard_map.101), channel_id=1, source_target_pairs={{0,16},{16,0},{1,17},{17,1},{2,18},{18,2},{3,19},{19,3},{4,20},{20... | collective-permute-start | bytes 3170312 | tf_op jit(solution)/shard_map/ppermute | solution.py:182

commit v5 on v4

--- a/solution.py
+++ b/solution.py
@@ -45,7 +45,7 @@
 
 
 def lag(me, amount):
-    @pl.when(me[0] == 0)
+    @pl.when(me == 0)
     def _():
         pl.delay(amount)
 
@@ -61,44 +61,51 @@
     return (col_tile // 2) % 4 * 4 + col_tile // 8
 
 
-def over_slots(count, near, order, step):
+def over_slots(near, plan, tiles, step):
+    n_far = plan[96]
+    count = plan[97] - n_far if near else n_far
+
     def group(g, carry):
         for k in range(UNROLL):
             i = g * UNROLL + k
-            step(order[31 - i if near else i], i < count)
+            p = 31 - i if near else i
+            tile = jnp.where(i < count, tiles[plan[p]], jnp.zeros((), BF16))
+            step(tile, plan[32 + p], plan[64 + p])
         return carry
 
     lax.fori_loop(0, (count + UNROLL - 1) // UNROLL, group, 0)
 
 
-def near_kernel(rows, cols, count, me, tiles, own, acc, order, far):
+def near_kernel(rows, cols, count, me, tiles, own, acc, plan):
+    mine = me[0]
+    for i in range(96):
+        plan[i] = 0
+
+    def place(s, n_far):
+        far = (cols[s] % 2 != mine).astype(jnp.int32)
+        p = jnp.where(far == 1, n_far, 31 - (s - n_far))
+        plan[p] = s
+        plan[32 + p] = rows[s]
+        plan[64 + p] = half_index(cols[s])
+        return n_far + far
+
+    plan[96] = lax.fori_loop(0, count[0], place, jnp.int32(0))
+    plan[97] = count[0]
+    plan[98] = mine
     acc[...] = jnp.zeros_like(acc)
-    mine = me[0]
-    for i in range(32):
-        order[i] = 0
-
-    def place(s, n_far):
-        is_far = (cols[s] % 2 != mine).astype(jnp.int32)
-        order[jnp.where(is_far == 1, n_far, 31 - (s - n_far))] = s
-        return n_far + is_far
-
-    n_far = lax.fori_loop(0, count[0], place, jnp.int32(0))
-    far[0] = n_far
-
-    def step(s, live):
-        tile = jnp.where(live, tiles[s], jnp.zeros((), BF16))
-        acc[rows[s]] += dot(tile, own[half_index(cols[s])], 1, 0)
-
-    over_slots(count[0] - n_far, True, order, step)
-
-
-def far_kernel(rows, cols, me, order, far, tiles, other, given, out, acc):
-    def step(s, live):
-        tile = jnp.where(live, tiles[s], jnp.zeros((), BF16))
-        acc[rows[s]] += dot(tile, other[half_index(cols[s])], 1, 0)
-
-    over_slots(far[0], False, order, step)
-    lag(me, LAG_F)
+
+    def step(tile, r, k):
+        acc[r] += dot(tile, own[k], 1, 0)
+
+    over_slots(True, plan, tiles, step)
+
+
+def far_kernel(plan, tiles, other, given, out, acc):
+    def step(tile, r, k):
+        acc[r] += dot(tile, other[k], 1, 0)
+
+    over_slots(False, plan, tiles, step)
+    lag(plan[98], LAG_F)
     out[...] = acc[...].astype(BF16)
 
 
@@ -135,23 +142,21 @@
         out[d, 4 * T :] = tail
 
 
-def backward_kernel(near, rows, cols, count, order, far, tiles, cots, out, acc):
+def backward_kernel(near, plan, tiles, cots, out, acc):
     acc[...] = jnp.zeros_like(acc)
 
-    def step(s, live):
-        r = rows[s]
+    def step(tile, r, k):
         source = cots[r // 4, pl.ds(pl.multiple_of(r % 4 * T, T), T)]
-        tile = jnp.where(live, tiles[s], jnp.zeros((), BF16))
-        acc[half_index(cols[s])] += dot(tile, source, 0, 0)
-
-    over_slots(count[0] - far[0] if near else far[0], near, order, step)
+        acc[k] += dot(tile, source, 0, 0)
+
+    over_slots(near, plan, tiles, step)
     for k in range(16):
         out[k * T : (k + 1) * T] = acc[k].astype(BF16)
     out[16 * T :] = total(cots, slice(4 * T, 4 * T + 16)).astype(BF16)
 
 
 def pack_y_kernel(me, own, got, out):
-    lag(me, LAG_B)
+    lag(me[0], LAG_B)
     for y in range(4):
         block = slice(y * 4 * T, (y + 1) * 4 * T)
         out[y, : 4 * T] = (own[block].astype(F32) + got[block].astype(F32)).astype(BF16)
@@ -192,21 +197,21 @@
     got = exchange(jnp.broadcast_to(features, (4, T, F)), "zl").reshape(4 * T, F)
     got = exchange(jnp.broadcast_to(got, (4, 4 * T, F)), "y").reshape(16, T, F)
     other = swap(got)
-    acc, order, far = call(
+    acc, plan = call(
         near_kernel,
-        (sds(16, T, F, dtype=F32), sds(32, dtype=jnp.int32), sds(1, dtype=jnp.int32)),
+        (sds(16, T, F, dtype=F32), sds(128, dtype=jnp.int32)),
         [SMEM] * 4 + [VMEM] * 2,
         (rows, cols, count, me, tiles, got),
         tile_flops,
-        out_specs=(VMEM, SMEM, SMEM),
+        out_specs=(VMEM, SMEM),
     )
     partial, _ = call(
         far_kernel,
         (sds(16, T, F), sds(16, T, F, dtype=F32)),
-        [SMEM] * 5 + [VMEM] * 3,
-        (rows, cols, me, order, far, tiles, other, acc),
+        [SMEM] + [VMEM] * 3,
+        (plan, tiles, other, acc),
         tile_flops,
-        aliases={7: 1},
+        aliases={3: 1},
     )
     parts = exchange(partial.reshape(4, 4 * T, F), "x")
     (summed,) = call(sum_kernel, (sds(4 * T, F),), [VMEM], (parts,), 2**20)
@@ -229,8 +234,8 @@
         call(
             functools.partial(backward_kernel, near),
             (sds(16 * T + 16, F),),
-            [SMEM] * 5 + [VMEM] * 2,
-            (rows, cols, count, order, far, tiles, cots),
+            [SMEM] + [VMEM] * 2,
+            (plan, tiles, cots),
             tile_flops,
             [pltpu.VMEM((16, T, F), F32)],
         )[0]

time: 177 us -> 175 us (0.989)
  Pallas kernels: 18.3 us -> 16.5 us
    pallas_call x11, Pallas kernels: 18.3 us -> 16.5 us  [call(): pl.pallas_call(kernel, out_shape=out_shapes, in_specs=in_specs, out_specs...]
where the time goes in v5:
time: 175 us
  blocking collectives  152 us (87%)
  Pallas kernels  16.5 us (9%)
  starting transfers between devices  3.83 us (2%)
    all_to_all x9, blocking collectives, exchange(): return lax.all_to_all(v, axis, 0, 0)  152 us
    pallas_call x11, Pallas kernels, call(): pl.pallas_call(kernel, out_shape=out_shapes, in_specs=in_specs, out_specs...  16.5 us
    ppermute x2, starting transfers between devices, swap(): return lax.ppermute(v, 'c', [(0, 1), (1, 0)])  3.83 us
  transfers between devices with their start and end apart: 2, of which 1 were waited for; matrix products, arithmetic and copies ran while one was open for 0% of the time, Pallas kernels for 3%

profile of v5, /device:TPU:2, one launch (start us, length us, event | category | flops | bytes accessed | tf_op | source)
XLA Modules:
  0.0 175.0 jit_solution(13119638811448786060)
XLA Ops:
  0.6 0.9 broadcast_in_dim.6
  1.5 14.6 %all_to_all.45 = bf16[4,128,256]{2,1,0:T(8,128)(2,1)S(1)} all-to-all(bf16[4,128,256]{2,1,0:T(8,128)(2,1)S(1)} %broadcast_in_dim.6), channel_id=1, replica_groups=mesh['zl'=4,'y'=4,'c'=2,'x'=4,'zh'=4] {'zl'}, dimensions={0} | all-to-all | bytes 524288 | tf_op jit(solution)/shard_map/all_to_all | solution.py:183
  16.1 0.1 broadcast_in_dim.7
  16.1 0.0 copy-start
  16.1 0.0 copy-start.3
  16.2 0.0 copy-start.4
  16.2 17.2 %all_to_all.46 = bf16[4,512,256]{2,1,0:T(8,128)(2,1)S(1)} all-to-all(bf16[4,512,256]{2,1,0:T(8,128)(2,1)S(1)} %broadcast_in_dim.7), channel_id=1, replica_groups=mesh['zl'=4,'y'=4,'c'=2,'x'=4,'zh'=4] {'y'}, dimensions={0} | all-to-all | bytes 2097152 | tf_op jit(solution)/shard_map/all_to_all | solution.py:183
  33.3 1.9 %collective-permute-start = (bf16[16,128,256]{2,1,0:T(8,128)(2,1)S(1)}, bf16[16,128,256]{2,1,0:T(8,128)(2,1)S(1)}, u32[]{:S(2)}, u32[]{:S(2)}) collective-permute-start(bf16[16,128,256]{2,1,0:T(8,128)(2,1)S(1)} %bitcast.15), channel_id=1, source_target_pairs={{0,16},{16,0},{1,17},{17,1},{2,18},{18,2},{3,19},{19,3},{4,20},{20... | collective-permute-start | bytes 3145736 | tf_op jit(solution)/shard_map/ppermute | solution.py:187
  35.9 0.0 copy-done
  35.9 0.0 copy-done.3
  35.9 0.0 copy-done.4
  35.9 2.9 %shard_map.94 = (f32[16,128,256]{2,1,0:T(8,128)S(1)}, s32[128]{0:T(128)S(1)}) custom-call(s32[32]{0:T(128)S(1)} %bitcast.20, s32[32]{0:T(128)S(1)} %bitcast.21, s32[1]{0:T(128)} %bitcast.10.count, s32[1]{0:T(128)} %bitcast.3.me, bf16[32,128,128]{2,1,0:T(8,128)(2,1)S(1)} %bitcast.11, bf16[16,128,256]{2,1,0:T(8,128)(2,1)S(1)} %bitcast.16), custom_call_target="tpu_custom_call" | custom-call | flops 268435456 | bytes 4195080 | tf_op jit(solution)/shard_map/pallas_call | solution.py:27
  38.8 0.0 collective-permute-done.other
  38.8 4.6 %shard_map.95 = (bf16[16,128,256]{2,1,0:T(8,128)(2,1)S(1)}, f32[16,128,256]{2,1,0:T(8,128)S(1)}) custom-call(s32[128]{0:T(128)S(1)} %get-tuple-element.11.plan, bf16[32,128,128]{2,1,0:T(8,128)(2,1)S(1)} %bitcast.12, bf16[16,128,256]{2,1,0:T(8,128)(2,1)S(1)} %collective-permute-done.other, ...), custom_call_target="tpu_custom_call", output_to_operand_aliasing={{1}: (3, {})} | custom-call | flops 268435456 | bytes 7340544 | tf_op jit(solution)/shard_map/pallas_call | solution.py:27
  43.4 15.7 %all_to_all.47.parts = bf16[4,512,256]{2,1,0:T(8,128)(2,1)S(1)} all-to-all(bf16[4,512,256]{2,1,0:T(8,128)(2,1)S(1)} %bitcast.18), channel_id=1, replica_groups=mesh['zl'=4,'y'=4,'c'=2,'x'=4,'zh'=4] {'x'}, dimensions={0} | all-to-all | bytes 2097152 | tf_op jit(solution)/shard_map/all_to_all | solution.py:183
  59.1 0.1 shard_map.96
  59.2 29.2 %all_to_all.48.parts = bf16[4,128,256]{2,1,0:T(8,128)(2,1)S(1)} all-to-all(bf16[4,128,256]{2,1,0:T(8,128)(2,1)S(1)} %bitcast.17), channel_id=1, replica_groups=mesh['zl'=4,'y'=4,'c'=2,'x'=4,'zh'=4] {'zh'}, dimensions={0} | all-to-all | bytes 524288 | tf_op jit(solution)/shard_map/all_to_all | solution.py:183
  88.5 0.0 copy-done.1
  88.5 0.9 shard_map.97
  89.3 14.0 %all_to_all.49.wparts = bf16[16,16,256]{2,1,0:T(8,128)(2,1)S(1)} all-to-all(bf16[16,16,256]{2,1,0:T(8,128)(2,1)S(1)} %bitcast.19), channel_id=1, replica_groups=mesh['zl'=4,'y'=4,'c'=2,'x'=4,'zh'=4] {'zl','y'}, dimensions={0} | all-to-all | bytes 262144 | tf_op jit(solution)/shard_map/all_to_all | solution.py:183
  103.4 19.1 %all_to_all.50.parts = bf16[4,144,256]{2,1,0:T(8,128)(2,1)S(1)} all-to-all(bf16[4,144,256]{2,1,0:T(8,128)(2,1)S(1)} %shard_map.98), channel_id=1, replica_groups=mesh['zl'=4,'y'=4,'c'=2,'x'=4,'zh'=4] {'zh'}, dimensions={0} | all-to-all | bytes 589824 | tf_op jit(solution)/shard_map/all_to_all | solution.py:183
  122.5 0.1 shard_map.99
  122.6 13.5 %all_to_all.51.cots = bf16[4,528,256]{2,1,0:T(8,128)(2,1)S(1)} all-to-all(bf16[4,528,256]{2,1,0:T(8,128)(2,1)S(1)} %shard_map.99), channel_id=1, replica_groups=mesh['zl'=4,'y'=4,'c'=2,'x'=4,'zh'=4] {'x'}, dimensions={0} | all-to-all | bytes 2162688 | tf_op jit(solution)/shard_map/all_to_all | solution.py:183
  136.0 1.8 %shard_map.101 = bf16[2064,256]{1,0:T(8,128)(2,1)S(1)} custom-call(s32[128]{0:T(128)S(1)} %get-tuple-element.11.plan, bf16[32,128,128]{2,1,0:T(8,128)(2,1)S(1)} %bitcast.13, bf16[4,528,256]{2,1,0:T(8,128)(2,1)S(1)} %all_to_all.51.cots), custom_call_target="tpu_custom_call" | custom-call | flops 268435456 | bytes 3187200 | tf_op jit(solution)/shard_map/pallas_call | solution.py:27
  137.9 1.9 %collective-permute-start.1 = (bf16[2064,256]{1,0:T(8,128)(2,1)S(1)}, bf16[2064,256]{1,0:T(8,128)(2,1)S(1)}, u32[]{:S(2)}, u32[]{:S(2)}) collective-permute-start(bf16[2064,256]{1,0:T(8,128)(2,1)S(1)} %shard_map.101), channel_id=1, source_target_pairs={{0,16},{16,0},{1,17},{17,1},{2,18},{18,2},{3,19},{19,3},{4,20},{20... | collective-permute-start | bytes 3170312 | tf_op jit(solution)/shard_map/ppermute | solution.py:187
  139.8 1.9 %shard_map.100.own = bf16[2064,256]{1,0:T(8,128)(2,1)S(1)} custom-call(s32[128]{0:T(128)S(1)} %get-tuple-element.11.plan, bf16[32,128,128]{2,1,0:T(8,128)(2,1)S(1)} %bitcast.14, bf16[4,528,256]{2,1,0:T(8,128)(2,1)S(1)} %all_to_all.51.cots), custom_call_target="tpu_custom_call" | custom-call | flops 268435456 | bytes 3187200 | tf_op jit(solution)/shard_map/pallas_call | solution.py:27
  141.7 0.8 collective-permute-done.1.got
  142.4 3.2 %shard_map.102 = bf16[4,528,256]{2,1,0:T(8,128)(2,1)S(1)} custom-call(s32[1]{0:T(128)} %bitcast.3.me, bf16[2064,256]{1,0:T(8,128)(2,1)S(1)} %shard_map.100.own, bf16[2064,256]{1,0:T(8,128)(2,1)S(1)} %collective-permute-done.1.got), custom_call_target="tpu_custom_call" | custom-call | flops 1048576 | bytes 3194884 | tf_op jit(solution)/shard_map/pallas_call | solution.py:27
  145.7 15.4 %all_to_all.52.parts = bf16[4,528,256]{2,1,0:T(8,128)(2,1)S(1)} all-to-all(bf16[4,528,256]{2,1,0:T(8,128)(2,1)S(1)} %shard_map.102), channel_id=1, replica_groups=mesh['zl'=4,'y'=4,'c'=2,'x'=4,'zh'=4] {'y'}, dimensions={0} | all-to-all | bytes 2162688 | tf_op jit(solution)/shard_map/all_to_all | solution.py:183
  161.1 0.1 shard_map.103
  161.2 12.9 %all_to_all.53.parts = bf16[4,192,256]{2,1,0:T(8,128)(2,1)S(1)} all-to-all(bf16[4,192,256]{2,1,0:T(8,128)(2,1)S(1)} %shard_map.103), channel_id=1, replica_groups=mesh['zl'=4,'y'=4,'c'=2,'x'=4,'zh'=4] {'zl'}, dimensions={0} | all-to-all | bytes 786432 | tf_op jit(solution)/shard_map/all_to_all | solution.py:183
  174.1 0.8 shard_map.104
  (4 shorter events, 0.0 us)
Async XLA Ops:
  16.1 19.8 %copy-start = (bf16[1,1,32,128,128]{4,3,2,1,0:T(8,128)(2,1)S(1)}, bf16[1,1,32,128,128]{4,3,2,1,0:T(8,128)(2,1)}, u32[]{:S(2)}) copy-start(bf16[1,1,32,128,128]{4,3,2,1,0:T(8,128)(2,1)} %param.8) | copy-start | bytes 3145732
  16.1 19.8 %copy-start.3 = (s32[1,1,32]{2,1,0:T(1,128)S(1)}, s32[1,1,32]{2,1,0:T(1,128)}, u32[]{:S(2)}) copy-start(s32[1,1,32]{2,1,0:T(1,128)} %param.9) | copy-start | bytes 388
  16.2 19.8 %copy-start.4 = (s32[1,1,32]{2,1,0:T(1,128)S(1)}, s32[1,1,32]{2,1,0:T(1,128)}, u32[]{:S(2)}) copy-start(s32[1,1,32]{2,1,0:T(1,128)} %param.10) | copy-start | bytes 388
  33.3 5.5 %collective-permute-start = (bf16[16,128,256]{2,1,0:T(8,128)(2,1)S(1)}, bf16[16,128,256]{2,1,0:T(8,128)(2,1)S(1)}, u32[]{:S(2)}, u32[]{:S(2)}) collective-permute-start(bf16[16,128,256]{2,1,0:T(8,128)(2,1)S(1)} %bitcast.15), channel_id=1, source_target_pairs={{0,16},{16,0},{1,17},{17,1},{2,18},{18,2},{3,19},{19,3},{4,20},{20... | collective-permute-start | bytes 3145736 | tf_op jit(solution)/shard_map/ppermute | solution.py:187
  59.1 29.4 %copy-start.1 = (bf16[256,256]{1,0:T(8,128)(2,1)S(1)}, bf16[256,256]{1,0:T(8,128)(2,1)}, u32[]{:S(2)}) copy-start(bf16[256,256]{1,0:T(8,128)(2,1)} %weight.3) | copy-start | bytes 393220
  59.1 29.4 %copy-start.2 = (bf16[128,256]{1,0:T(8,128)(2,1)S(1)}, bf16[128,256]{1,0:T(8,128)(2,1)}, u32[]{:S(2)}) copy-start(bf16[128,256]{1,0:T(8,128)(2,1)} %upstream.1) | copy-start | bytes 196612
  137.9 4.6 %collective-permute-start.1 = (bf16[2064,256]{1,0:T(8,128)(2,1)S(1)}, bf16[2064,256]{1,0:T(8,128)(2,1)S(1)}, u32[]{:S(2)}, u32[]{:S(2)}) collective-permute-start(bf16[2064,256]{1,0:T(8,128)(2,1)S(1)} %shard_map.101), channel_id=1, source_target_pairs={{0,16},{16,0},{1,17},{17,1},{2,18},{18,2},{3,19},{19,3},{4,20},{20... | collective-permute-start | bytes 3170312 | tf_op jit(solution)/shard_map/ppermute | solution.py:187

commit v6 on v3

--- a/solution.py
+++ b/solution.py
@@ -13,7 +13,7 @@
 SIZES = (4, 4, 2, 4, 4)
 T = 128
 F = 256
-UNROLL = 4
+UNROLL = 8
 LAG_F = 3000
 LAG_B = 3000
 WHO = 0

time: 175 us -> 175 us (level)
  no operation moved by 1% of the time
where the time goes in v6:
time: 175 us; the launch traced here: 174 us
  blocking collectives  150 us (86%)
  Pallas kernels  12.9 us (7%)
  waiting for transfers between devices  4.61 us (3%)
  starting transfers between devices  3.83 us (2%)
    all_to_all x9, blocking collectives, exchange(): return lax.all_to_all(v, axis, 0, 0)  150 us
    pallas_call x9, Pallas kernels, call(): pl.pallas_call(kernel, out_shape=out_shapes, in_specs=in_specs, out_specs...  12.9 us
    ppermute x2, waiting for transfers between devices, swap(): return lax.ppermute(v, 'c', [(0, 1), (1, 0)])  4.61 us
    ppermute x2, starting transfers between devices, swap(): return lax.ppermute(v, 'c', [(0, 1), (1, 0)])  3.83 us
  transfers between devices with their start and end apart: 2, of which 2 were waited for; matrix products, arithmetic and copies ran while one was open for 0% of the time, Pallas kernels for 0%

profile of v6, /device:TPU:2, one launch (start us, length us, event | category | flops | bytes accessed | tf_op | source)
XLA Modules:
  0.0 173.8 jit_solution(2979864756195663071)
XLA Ops:
  0.6 0.9 broadcast_in_dim.6
  1.5 14.6 %all_to_all.45 = bf16[4,128,256]{2,1,0:T(8,128)(2,1)S(1)} all-to-all(bf16[4,128,256]{2,1,0:T(8,128)(2,1)S(1)} %broadcast_in_dim.6), channel_id=1, replica_groups=mesh['zl'=4,'y'=4,'c'=2,'x'=4,'zh'=4] {'zl'}, dimensions={0} | all-to-all | bytes 524288 | tf_op jit(solution)/shard_map/all_to_all | solution.py:170
  16.1 0.1 broadcast_in_dim.7
  16.1 0.0 copy-start
  16.1 0.0 copy-start.3
  16.2 0.0 copy-start.4
  16.2 17.2 %all_to_all.46 = bf16[4,512,256]{2,1,0:T(8,128)(2,1)S(1)} all-to-all(bf16[4,512,256]{2,1,0:T(8,128)(2,1)S(1)} %broadcast_in_dim.7), channel_id=1, replica_groups=mesh['zl'=4,'y'=4,'c'=2,'x'=4,'zh'=4] {'y'}, dimensions={0} | all-to-all | bytes 2097152 | tf_op jit(solution)/shard_map/all_to_all | solution.py:170
  33.3 1.9 %collective-permute-start = (bf16[16,128,256]{2,1,0:T(8,128)(2,1)S(1)}, bf16[16,128,256]{2,1,0:T(8,128)(2,1)S(1)}, u32[]{:S(2)}, u32[]{:S(2)}) collective-permute-start(bf16[16,128,256]{2,1,0:T(8,128)(2,1)S(1)} %bitcast.14), channel_id=1, source_target_pairs={{0,16},{16,0},{1,17},{17,1},{2,18},{18,2},{3,19},{19,3},{4,20},{20... | collective-permute-start | bytes 3145736 | tf_op jit(solution)/shard_map/ppermute | solution.py:174
  35.9 2.0 %collective-permute-done.other = bf16[16,128,256]{2,1,0:T(8,128)(2,1)S(1)} collective-permute-done((bf16[16,128,256]{2,1,0:T(8,128)(2,1)S(1)}, bf16[16,128,256]{2,1,0:T(8,128)(2,1)S(1)}, u32[]{:S(2)}, u32[]{:S(2)}) %collective-permute-start) | collective-permute-done | bytes 1048608 | tf_op jit(solution)/shard_map/ppermute | solution.py:174
  37.9 0.0 copy-done
  37.9 0.0 copy-done.3
  37.9 0.0 copy-done.4
  37.9 5.0 %shard_map.94 = bf16[16,128,256]{2,1,0:T(8,128)(2,1)S(1)} custom-call(s32[32]{0:T(128)S(1)} %bitcast.19, s32[32]{0:T(128)S(1)} %bitcast.21, s32[1]{0:T(128)} %bitcast.10.count, s32[1]{0:T(128)} %bitcast.3.me, bf16[32,128,128]{2,1,0:T(8,128)(2,1)S(1)} %bitcast.12, bf16[16,128,256]{2,1,0:T(8,128)(2,1)S(1)} %bitcast.15, ...), custom_call_target="tpu_custom_call" | custom-call | flops 268435456 | bytes 4194568 | tf_op jit(solution)/shard_map/pallas_call | solution.py:28
  42.9 15.3 %all_to_all.47.parts = bf16[4,512,256]{2,1,0:T(8,128)(2,1)S(1)} all-to-all(bf16[4,512,256]{2,1,0:T(8,128)(2,1)S(1)} %bitcast.16), channel_id=1, replica_groups=mesh['zl'=4,'y'=4,'c'=2,'x'=4,'zh'=4] {'x'}, dimensions={0} | all-to-all | bytes 2097152 | tf_op jit(solution)/shard_map/all_to_all | solution.py:170
  58.2 0.0 copy-start.1
  58.2 0.1 shard_map.95
  58.4 29.2 %all_to_all.48.parts = bf16[4,128,256]{2,1,0:T(8,128)(2,1)S(1)} all-to-all(bf16[4,128,256]{2,1,0:T(8,128)(2,1)S(1)} %bitcast.17), channel_id=1, replica_groups=mesh['zl'=4,'y'=4,'c'=2,'x'=4,'zh'=4] {'zh'}, dimensions={0} | all-to-all | bytes 524288 | tf_op jit(solution)/shard_map/all_to_all | solution.py:170
  87.6 0.0 copy-done.1
  87.6 0.0 copy-done.2
  87.6 0.9 shard_map.96
  88.5 13.2 %all_to_all.49.wparts = bf16[16,16,256]{2,1,0:T(8,128)(2,1)S(1)} all-to-all(bf16[16,16,256]{2,1,0:T(8,128)(2,1)S(1)} %bitcast.18), channel_id=1, replica_groups=mesh['zl'=4,'y'=4,'c'=2,'x'=4,'zh'=4] {'zl','y'}, dimensions={0} | all-to-all | bytes 262144 | tf_op jit(solution)/shard_map/all_to_all | solution.py:170
  101.7 19.5 %all_to_all.50.parts = bf16[4,144,256]{2,1,0:T(8,128)(2,1)S(1)} all-to-all(bf16[4,144,256]{2,1,0:T(8,128)(2,1)S(1)} %shard_map.97), channel_id=1, replica_groups=mesh['zl'=4,'y'=4,'c'=2,'x'=4,'zh'=4] {'zh'}, dimensions={0} | all-to-all | bytes 589824 | tf_op jit(solution)/shard_map/all_to_all | solution.py:170
  121.2 0.1 shard_map.98
  121.3 13.5 %all_to_all.51.cots = bf16[4,528,256]{2,1,0:T(8,128)(2,1)S(1)} all-to-all(bf16[4,528,256]{2,1,0:T(8,128)(2,1)S(1)} %shard_map.98), channel_id=1, replica_groups=mesh['zl'=4,'y'=4,'c'=2,'x'=4,'zh'=4] {'x'}, dimensions={0} | all-to-all | bytes 2162688 | tf_op jit(solution)/shard_map/all_to_all | solution.py:170
  134.7 2.6 %shard_map.99 = (bf16[2064,256]{1,0:T(8,128)(2,1)S(1)}, bf16[2064,256]{1,0:T(8,128)(2,1)S(1)}) custom-call(s32[32]{0:T(128)S(1)} %bitcast.20, s32[32]{0:T(128)S(1)} %bitcast.22, s32[1]{0:T(128)} %bitcast.11.count, s32[1]{0:T(128)} %bitcast.3.me, bf16[32,128,128]{2,1,0:T(8,128)(2,1)S(1)} %bitcast.13, bf16[4,528,256]{2,1,0:T(8,128)(2,1)S(1)} %all_to_all.51.cots), custom_call_target="tpu_custom_call" | custom-call | flops 268435456 | bytes 4243720 | tf_op jit(solution)/shard_map/pallas_call | solution.py:28
  137.3 1.9 %collective-permute-start.1 = (bf16[2064,256]{1,0:T(8,128)(2,1)S(1)}, bf16[2064,256]{1,0:T(8,128)(2,1)S(1)}, u32[]{:S(2)}, u32[]{:S(2)}) collective-permute-start(bf16[2064,256]{1,0:T(8,128)(2,1)S(1)} %get-tuple-element.14), channel_id=1, source_target_pairs={{0,16},{16,0},{1,17},{17,1},{2,18},{18,2},{3,19},{19,3},{4,20},{20... | collective-permute-start | bytes 3170312 | tf_op jit(solution)/shard_map/ppermute | solution.py:174
  139.2 2.6 %collective-permute-done.1.got = bf16[2064,256]{1,0:T(8,128)(2,1)S(1)} collective-permute-done((bf16[2064,256]{1,0:T(8,128)(2,1)S(1)}, bf16[2064,256]{1,0:T(8,128)(2,1)S(1)}, u32[]{:S(2)}, u32[]{:S(2)}) %collective-permute-start.1) | collective-permute-done | bytes 1056800 | tf_op jit(solution)/shard_map/ppermute | solution.py:174
  141.9 3.2 %shard_map.100 = bf16[4,528,256]{2,1,0:T(8,128)(2,1)S(1)} custom-call(s32[1]{0:T(128)} %bitcast.3.me, bf16[2064,256]{1,0:T(8,128)(2,1)S(1)} %get-tuple-element.13.own, bf16[2064,256]{1,0:T(8,128)(2,1)S(1)} %collective-permute-done.1.got), custom_call_target="tpu_custom_call" | custom-call | flops 1048576 | bytes 3194884 | tf_op jit(solution)/shard_map/pallas_call | solution.py:28
  145.1 15.4 %all_to_all.52.parts = bf16[4,528,256]{2,1,0:T(8,128)(2,1)S(1)} all-to-all(bf16[4,528,256]{2,1,0:T(8,128)(2,1)S(1)} %shard_map.100), channel_id=1, replica_groups=mesh['zl'=4,'y'=4,'c'=2,'x'=4,'zh'=4] {'y'}, dimensions={0} | all-to-all | bytes 2162688 | tf_op jit(solution)/shard_map/all_to_all | solution.py:170
  160.5 0.1 shard_map.101
  160.7 12.3 %all_to_all.53.parts = bf16[4,192,256]{2,1,0:T(8,128)(2,1)S(1)} all-to-all(bf16[4,192,256]{2,1,0:T(8,128)(2,1)S(1)} %shard_map.101), channel_id=1, replica_groups=mesh['zl'=4,'y'=4,'c'=2,'x'=4,'zh'=4] {'zl'}, dimensions={0} | all-to-all | bytes 786432 | tf_op jit(solution)/shard_map/all_to_all | solution.py:170
  173.0 0.8 shard_map.102
  (2 shorter events, 0.0 us)
Async XLA Ops:
  16.1 21.7 %copy-start = (bf16[1,1,32,128,128]{4,3,2,1,0:T(8,128)(2,1)S(1)}, bf16[1,1,32,128,128]{4,3,2,1,0:T(8,128)(2,1)}, u32[]{:S(2)}) copy-start(bf16[1,1,32,128,128]{4,3,2,1,0:T(8,128)(2,1)} %param.8) | copy-start | bytes 3145732
  16.1 21.7 %copy-start.3 = (s32[1,1,32]{2,1,0:T(1,128)S(1)}, s32[1,1,32]{2,1,0:T(1,128)}, u32[]{:S(2)}) copy-start(s32[1,1,32]{2,1,0:T(1,128)} %param.9) | copy-start | bytes 388
  16.2 21.7 %copy-start.4 = (s32[1,1,32]{2,1,0:T(1,128)S(1)}, s32[1,1,32]{2,1,0:T(1,128)}, u32[]{:S(2)}) copy-start(s32[1,1,32]{2,1,0:T(1,128)} %param.10) | copy-start | bytes 388
  33.3 4.5 %collective-permute-start = (bf16[16,128,256]{2,1,0:T(8,128)(2,1)S(1)}, bf16[16,128,256]{2,1,0:T(8,128)(2,1)S(1)}, u32[]{:S(2)}, u32[]{:S(2)}) collective-permute-start(bf16[16,128,256]{2,1,0:T(8,128)(2,1)S(1)} %bitcast.14), channel_id=1, source_target_pairs={{0,16},{16,0},{1,17},{17,1},{2,18},{18,2},{3,19},{19,3},{4,20},{20... | collective-permute-start | bytes 3145736 | tf_op jit(solution)/shard_map/ppermute | solution.py:174
  58.2 29.4 %copy-start.1 = (bf16[256,256]{1,0:T(8,128)(2,1)S(1)}, bf16[256,256]{1,0:T(8,128)(2,1)}, u32[]{:S(2)}) copy-start(bf16[256,256]{1,0:T(8,128)(2,1)} %weight.3) | copy-start | bytes 393220
  58.2 29.4 %copy-start.2 = (bf16[128,256]{1,0:T(8,128)(2,1)S(1)}, bf16[128,256]{1,0:T(8,128)(2,1)}, u32[]{:S(2)}) copy-start(bf16[128,256]{1,0:T(8,128)(2,1)} %upstream.1) | copy-start | bytes 196612
  137.3 4.6 %collective-permute-start.1 = (bf16[2064,256]{1,0:T(8,128)(2,1)S(1)}, bf16[2064,256]{1,0:T(8,128)(2,1)S(1)}, u32[]{:S(2)}, u32[]{:S(2)}) collective-permute-start(bf16[2064,256]{1,0:T(8,128)(2,1)S(1)} %get-tuple-element.14), channel_id=1, source_target_pairs={{0,16},{16,0},{1,17},{17,1},{2,18},{18,2},{3,19},{19,3},{4,20},{20... | collective-permute-start | bytes 3170312 | tf_op jit(solution)/shard_map/ppermute | solution.py:174
